TPU v7x, 32 devices: a whole 2x2x4 slice. The times are simulated.
32 devices in a mesh: ctx: 4 (over x, core), exp: 8 (over z, y).
Axes of the slice: x: 2, y: 2, z: 4, core: 2. Of those that a mesh axis runs over, the one named last changes fastest.
Arguments:
- queries: bfloat16 [8, 512, 1536], P('exp', 'ctx'), may hold values from -2.5 to 2.5
- key_states: bfloat16 [8, 512, 1536], P('exp', 'ctx'), may hold values from -2.5 to 2.5
- value_states: bfloat16 [8, 512, 1536], P('exp', 'ctx'), may hold values from -6 to 6
- attended: bfloat16 [8, 512, 1536], P('exp', 'ctx'), may hold values from -6 to 6
- output_grad: bfloat16 [8, 512, 1536], P('exp', 'ctx'), may hold values from -6 to 6
- expert_ids: int32 [8, 512, 2], P('exp', 'ctx'), may hold values from 0 to 7, all different within a row; in each aligned block of 128 rows (0 to 127, 128 to 255, ..., all dimensions but the last counted through in order) at most 48 rows name the same one
- gate_weights: float32 [8, 512, 2], P('exp', 'ctx'), may hold values from 0.2 to 1
- w_in: bfloat16 [8, 1536, 768], P('exp'), may hold values from -0.15625 to 0.15625
- w_out: bfloat16 [8, 768, 1536], P('exp'), may hold values from -0.21875 to 0.21875
Outputs:
- query_grad: bfloat16 [8, 512, 1536], P('exp', 'ctx')
- key_grad: bfloat16 [8, 512, 1536], P('exp', 'ctx')
- value_grad: bfloat16 [8, 512, 1536], P('exp', 'ctx')
- w_in_grad: bfloat16 [8, 1536, 768], P('exp', 'ctx')
- w_out_grad: bfloat16 [8, 768, 1536], P('exp', 'ctx')
Inputs may be any that keep to these rules, and one draw needn't show every extreme that they name: `expert_ids`: in each aligned block of 128 frames (the frames of one device) no expert is named by more than 48 frames, a bound that some block reaches; the two experts of a frame differ.
All inputs are finite; a program needn't handle non-finite values.
Results may differ from a plain program's by a relative error of at most 0.02.
Values may be sent and summed in bfloat16 or wider, within the bound.
No kernel may reach another device: no remote copies, remote signals or barrier semaphores. Data moves between devices by JAX's collectives and lax.ppermute only.
A program may use at most 128 MiB of HBM per device.

v0:
```python
import jax
import jax.numpy as jnp
from jax import lax
from jax.sharding import PartitionSpec as P

HEAD_DIM = 128
EXP_DEV = 1


def rounded(x):
    return lax.optimization_barrier(x.astype(jnp.bfloat16)).astype(jnp.float32)


def per_device(
    queries, key_states, value_states, attended, output_grad, expert_ids, gate_weights, w_in, w_out
):
    tok = queries.shape[1]
    width = queries.shape[2]
    heads = width // HEAD_DIM
    nexp = lax.axis_size("exp")
    nctx = lax.axis_size("ctx")
    experts = EXP_DEV * nexp
    capacity = 3 * tok // experts
    attn_rows = attended[0]
    grad_rows = output_grad[0]
    route = expert_ids[0].reshape(-1)
    gates = gate_weights[0].reshape(-1)
    onehot = (route[:, None] == jnp.arange(experts, dtype=jnp.int32)[None, :]).astype(jnp.int32)
    slots = jnp.sum((jnp.cumsum(onehot, axis=0) - 1) * onehot, axis=1)
    target = route * capacity + slots
    placed = target[None, :] == jnp.arange(experts * capacity, dtype=jnp.int32)[:, None]
    picker = (
        placed.reshape(experts * capacity, tok, 2)
        .astype(jnp.float32)
        .sum(axis=2)
        .astype(jnp.bfloat16)
    )
    slot_gate = jnp.sum(jnp.where(placed, gates[None, :], 0.0), axis=1)
    sent_rows = jnp.dot(picker, attn_rows, preferred_element_type=jnp.float32).astype(jnp.bfloat16)
    sent_grads = (
        jnp.dot(picker, grad_rows, preferred_element_type=jnp.float32) * slot_gate[:, None]
    ).astype(jnp.bfloat16)
    shape = (nexp, EXP_DEV * capacity, width)
    got_rows, got_grads = (
        lax.all_to_all(sent_rows.reshape(shape), "exp", split_axis=0, concat_axis=0, tiled=True),
        lax.all_to_all(sent_grads.reshape(shape), "exp", split_axis=0, concat_axis=0, tiled=True),
    )

    def by_expert(values):
        return (
            values.reshape(nexp, EXP_DEV, capacity, -1)
            .transpose(1, 0, 2, 3)
            .reshape(EXP_DEV, nexp * capacity, -1)
        )

    rows_in = by_expert(got_rows)
    grads_in = by_expert(got_grads)
    upper = jnp.einsum("erd,edf->erf", rows_in, w_in, preferred_element_type=jnp.float32)
    sig = jax.nn.sigmoid(upper)
    act = (upper * sig).astype(jnp.bfloat16)
    act_grad = jnp.einsum("erd,efd->erf", grads_in, w_out, preferred_element_type=jnp.float32)
    up_grad = (act_grad * sig * (1.0 + upper * (1.0 - sig))).astype(jnp.bfloat16)
    row_back = jnp.einsum("erf,edf->erd", up_grad, w_in, preferred_element_type=jnp.float32).astype(
        jnp.bfloat16
    )
    first_term = jnp.einsum("erd,erf->edf", rows_in, up_grad, preferred_element_type=jnp.float32)
    second_term = jnp.einsum("erf,erd->efd", act, grads_in, preferred_element_type=jnp.float32)
    back_send = (
        row_back.reshape(EXP_DEV, nexp, capacity, width).transpose(1, 0, 2, 3).reshape(shape)
    )
    returned = lax.all_to_all(back_send, "exp", split_axis=0, concat_axis=0, tiled=True)
    back_sum = jnp.dot(
        picker.T, returned.reshape(experts * capacity, width), preferred_element_type=jnp.float32
    )
    attn_grad = (grad_rows.astype(jnp.float32) + back_sum).astype(jnp.bfloat16)
    first_sum, second_sum = (
        lax.psum_scatter(
            first_term.astype(jnp.bfloat16), "ctx", scatter_dimension=1, tiled=True
        ).astype(jnp.float32),
        lax.psum_scatter(
            second_term.astype(jnp.bfloat16), "ctx", scatter_dimension=1, tiled=True
        ).astype(jnp.float32),
    )
    w_in_grad = first_sum.astype(jnp.bfloat16)
    w_out_grad = second_sum.astype(jnp.bfloat16)
    scale = HEAD_DIM ** (-0.5)
    group = min(max(1, 512 // tok), nctx)
    blocks = nctx // group
    key_heads = key_states[0].reshape(tok, heads, HEAD_DIM)
    value_heads = value_states[0].reshape(tok, heads, HEAD_DIM)
    delta = jnp.sum(
        (attn_grad.astype(jnp.float32) * attn_rows.astype(jnp.float32)).reshape(
            tok, heads, HEAD_DIM
        ),
        axis=2,
    )
    query_all, grad_all = (
        lax.all_gather(queries[0], "ctx", axis=0, tiled=True),
        lax.all_gather(attn_grad, "ctx", axis=0, tiled=True),
    )
    span = group * tok
    query_blocks = query_all.reshape(blocks, span, heads, HEAD_DIM)
    grad_blocks = grad_all.reshape(blocks, span, heads, HEAD_DIM)

    def norm_part(carry, query_blk):
        scores = (
            jnp.einsum("qhd,khd->hqk", query_blk, key_heads, preferred_element_type=jnp.float32)
            * scale
        )
        return (carry, jnp.sum(jnp.exp(scores), axis=2).T)

    _, partial_sums = lax.scan(norm_part, jnp.zeros((), jnp.float32), query_blocks)
    own_delta = jnp.zeros((nctx * tok, heads), jnp.float32)
    own_delta = lax.dynamic_update_slice(own_delta, delta, (lax.axis_index("ctx") * tok, 0))
    totals, delta_all = (
        lax.psum(partial_sums.reshape(nctx * tok, heads).astype(jnp.bfloat16), "ctx").astype(
            jnp.float32
        ),
        lax.psum(own_delta.astype(jnp.bfloat16), "ctx").astype(jnp.float32),
    )
    norm_blocks = jnp.log(totals).reshape(blocks, span, heads)
    delta_blocks = delta_all.reshape(blocks, span, heads)

    def grad_step(carry, blk):
        key_acc, value_acc = carry
        query_blk, grad_blk, norm_blk, delta_blk = blk
        scores = (
            jnp.einsum("qhd,khd->hqk", query_blk, key_heads, preferred_element_type=jnp.float32)
            * scale
        )
        probs = jnp.exp(scores - norm_blk.T[:, :, None])
        probs_b = probs.astype(jnp.bfloat16)
        prob_grad = jnp.einsum(
            "qhd,khd->hqk", grad_blk, value_heads, preferred_element_type=jnp.float32
        )
        score_grad = (probs * (prob_grad - delta_blk.T[:, :, None])).astype(jnp.bfloat16)
        query_term = (
            jnp.einsum("hqk,khd->qhd", score_grad, key_heads, preferred_element_type=jnp.float32)
            * scale
        )
        split_grad = score_grad.reshape(heads, group, tok, tok)
        split_probs = probs_b.reshape(heads, group, tok, tok)
        split_query = query_blk.reshape(group, tok, heads, HEAD_DIM)
        split_out = grad_blk.reshape(group, tok, heads, HEAD_DIM)
        key_part = (
            jnp.einsum(
                "hgqk,gqhd->gkhd", split_grad, split_query, preferred_element_type=jnp.float32
            )
            * scale
        )
        value_part = jnp.einsum(
            "hgqk,gqhd->gkhd", split_probs, split_out, preferred_element_type=jnp.float32
        )
        key_acc = key_acc + jnp.sum(rounded(key_part), axis=0)
        value_acc = value_acc + jnp.sum(rounded(value_part), axis=0)
        return ((key_acc, value_acc), query_term)

    zero = jnp.zeros((tok, heads, HEAD_DIM), jnp.float32)
    (key_acc, value_acc), query_terms = lax.scan(
        grad_step, (zero, zero), (query_blocks, grad_blocks, norm_blocks, delta_blocks)
    )
    query_sum = lax.psum_scatter(
        query_terms.reshape(nctx * tok, width).astype(jnp.bfloat16),
        "ctx",
        scatter_dimension=0,
        tiled=True,
    )
    key_grad = key_acc.reshape(tok, width).astype(jnp.bfloat16)
    value_grad = value_acc.reshape(tok, width).astype(jnp.bfloat16)
    return (query_sum[None], key_grad[None], value_grad[None], w_in_grad, w_out_grad)


def solution(mesh):
    return jax.shard_map(
        per_device,
        mesh=mesh,
        in_specs=(
            P("exp", "ctx", None),
            P("exp", "ctx", None),
            P("exp", "ctx", None),
            P("exp", "ctx", None),
            P("exp", "ctx", None),
            P("exp", "ctx", None),
            P("exp", "ctx", None),
            P("exp", None, None),
            P("exp", None, None),
        ),
        out_specs=(
            P("exp", "ctx", None),
            P("exp", "ctx", None),
            P("exp", "ctx", None),
            P("exp", "ctx", None),
            P("exp", "ctx", None),
        ),
        check_vma=False,
    )
```

profile of v0, /device:TPU:0, one launch (start us, length us, event | category | flops | bytes accessed | tf_op | source)
XLA Modules:
  0.0 263.2 jit_solution(12202675139795974552)
XLA Ops:
  7.2 0.9 copy.74
  8.4 0.6 reduce-window.6
  9.0 0.2 slice_reduce_fusion
  9.7 2.5 convolution_convert_fusion.2
  12.2 7.4 %all-to-all-start.1 = ((bf16[8,48,1536]{2,1,0:T(8,128)(2,1)}), bf16[8,48,1536]{2,1,0:T(8,128)(2,1)}, u32[]{:S(2)}, u32[]{:S(2)}) async-start(bf16[8,48,1536]{2,1,0:T(8,128)(2,1)} %bitcast.12), calls=%async_computation.1 | async-start | bytes 2359296 | tf_op jit(solution)/shard_map/all_to_all | solution.py:45
  20.1 1.5 fusion.2
  21.5 26.8 %all-to-all-done.1 = bf16[8,48,1536]{2,1,0:T(8,128)(2,1)} async-done(((bf16[8,48,1536]{2,1,0:T(8,128)(2,1)}), bf16[8,48,1536]{2,1,0:T(8,128)(2,1)}, u32[]{:S(2)}, u32[]{:S(2)}) %all-to-all-start.1) | async-done | bytes 1179680 | tf_op jit(solution)/shard_map/all_to_all | solution.py:45
  48.3 3.6 %all-to-all-start = ((bf16[8,48,1536]{2,1,0:T(8,128)(2,1)}), bf16[8,48,1536]{2,1,0:T(8,128)(2,1)S(1)}, u32[]{:S(2)}, u32[]{:S(2)}) async-start(bf16[8,48,1536]{2,1,0:T(8,128)(2,1)} %bitcast.8), calls=%async_computation | async-start | bytes 2359296 | tf_op jit(solution)/shard_map/all_to_all | solution.py:46
  52.0 3.4 %fusion.6 = f32[384,768]{1,0:T(8,128)} fusion(bf16[384,1536]{1,0:T(8,128)(2,1)} %bitcast.13, bf16[1,1536,768]{2,1,0:T(8,128)(2,1)S(1)} %copy-done), kind=kOutput, calls=%fused_computation.17 | convolution fusion | flops 905969664 | bytes 4718592 | tf_op jit(solution)/shard_map/erd,edf->erf/dot_general | solution.py:58
  55.4 25.4 %all-to-all-done = bf16[8,48,1536]{2,1,0:T(8,128)(2,1)S(1)} async-done(((bf16[8,48,1536]{2,1,0:T(8,128)(2,1)}), bf16[8,48,1536]{2,1,0:T(8,128)(2,1)S(1)}, u32[]{:S(2)}, u32[]{:S(2)}) %all-to-all-start) | async-done | bytes 1179680 | tf_op jit(solution)/shard_map/all_to_all | solution.py:46
  80.7 3.6 %fusion.31 = bf16[384,768]{1,0:T(8,128)(2,1)S(1)} fusion(bf16[384,1536]{1,0:T(8,128)(2,1)S(1)} %bitcast.97, bf16[1,768,1536]{2,1,0:T(8,128)(2,1)} %param.17, f32[384,768]{1,0:T(8,128)} %fusion.6), kind=kOutput, calls=%fused_computation.31 | convolution fusion | flops 908623872 | bytes 5308416 | tf_op jit(solution)/shard_map/erd,efd->erf/dot_general | solution.py:61
  84.4 2.2 convolution_convert_fusion.3
  86.6 3.6 %all-to-all-start.2 = ((bf16[8,48,1536]{2,1,0:T(8,128)(2,1)}), bf16[8,48,1536]{2,1,0:T(8,128)(2,1)S(1)}, u32[]{:S(2)}, u32[]{:S(2)}) async-start(bf16[8,48,1536]{2,1,0:T(8,128)(2,1)} %bitcast.99), calls=%async_computation.2 | async-start | bytes 2359296 | tf_op jit(solution)/shard_map/all_to_all | solution.py:71
  90.3 1.9 copy.70
  92.3 26.7 %all-to-all-done.2 = bf16[8,48,1536]{2,1,0:T(8,128)(2,1)S(1)} async-done(((bf16[8,48,1536]{2,1,0:T(8,128)(2,1)}), bf16[8,48,1536]{2,1,0:T(8,128)(2,1)S(1)}, u32[]{:S(2)}, u32[]{:S(2)}) %all-to-all-start.2) | async-done | bytes 1179680 | tf_op jit(solution)/shard_map/all_to_all | solution.py:71
  119.0 2.6 %convert_multiply_fusion = (f32[128,1536]{1,0:T(8,128)}, bf16[128,1536]{1,0:T(8,128)(2,1)}) fusion(bf16[1,128,1536]{2,1,0:T(8,128)(2,1)} %param.12, bf16[384,128]{1,0:T(8,128)(2,1)} %copy-done.2, bf16[384,1536]{1,0:T(8,128)(2,1)S(1)} %bitcast.89, bf16[1,128,1536]{2,1,0:T(8,128)(2,1)} %param.13), kind=kOutput, calls=%fused_computation.34 | convolution fusion | flops 152174592 | bytes 3244032 | tf_op jit(solution)/shard_map/dot_general | solution.py:72
  121.8 1.2 copy.71
  123.0 1.9 copy.80
  124.9 3.8 %exponential_reduce_fusion = (bf16[12,512]{1,0:T(8,128)(2,1)S(1)}, f32[12,512,128]{2,1,0:T(8,128)}) fusion(bf16[512,12,128]{0,2,1:T(8,128)(2,1)} %bitcast.86, bf16[128,12,128]{0,2,1:T(8,128)(2,1)S(1)} %bitcast.90), kind=kOutput, calls=%fused_computation.6 | convolution fusion | flops 202893312 | bytes 5124096 | tf_op jit(solution)/shard_map/while/body/eval_jaxpr/qhd,khd->hqk/dot_general | solution.py:128
  128.7 1.4 copy.83
  130.1 0.7 reduce_sum.79
  130.8 0.7 constant_dynamic-update-slice_fusion
  131.5 11.3 %all-reduce = (bf16[12,512]{1,0:T(8,128)(2,1)S(1)}, bf16[512,12]{0,1:T(8,128)(2,1)S(1)}) all-reduce(bf16[12,512]{1,0:T(8,128)(2,1)S(1)} %bitcast.101, bf16[512,12]{0,1:T(8,128)(2,1)S(1)} %bitcast.100), channel_id=1, replica_groups=mesh['ctx'=4,'exp'=8] {'ctx'}, use_global_device_ids=true, to_apply=%region_8.9 | all-reduce | flops 12288 | bytes 49152 | tf_op jit(solution)/shard_map/psum | solution.py:119
  142.9 2.6 %copy.79 = bf16[512,1536]{0,1:T(8,128)(2,1)} copy(bf16[512,1536]{1,0:T(8,128)(2,1)} %all-gather.4.cloned.1.call-done) | data formatting | bytes 3145728 | tf_op jit(solution)/shard_map/all_gather | solution.py:99
  145.5 3.9 %multiply_convert_fusion.2 = bf16[12,512,128]{2,1,0:T(8,128)(2,1)S(1)} fusion(f32[12,512,128]{2,1,0:T(8,128)} %get-tuple-element.67, bf16[512,12,128]{0,2,1:T(8,128)(2,1)} %bitcast.87, bf16[128,12,128]{0,2,1:T(8,128)(2,1)S(1)} %bitcast.93, f32[12,512]{1,0:T(8,128)S(1)} %transpose.60, f32[12,512]{1,0:T(8,128)S(1)} %log_bitcast_fusion), kind=kOutput, calls=%fused_computation.4 | convolution fusion | flops 205258752 | bytes 6733824 | tf_op jit(solution)/shard_map/while/body/eval_jaxpr/qhd,khd->hqk/dot_general | solution.py:133
  149.4 1.2 copy-done.1
  150.6 1.7 fusion.24
  152.4 2.6 copy.85
  154.9 2.6 copy.104
  157.6 1.2 copy-done.6
  158.8 4.2 %fusion.1 = bf16[1,768,1536]{2,1,0:T(8,128)(2,1)} fusion(bf16[384,1536]{1,0:T(8,128)(2,1)S(1)} %bitcast.98, f32[384,768]{1,0:T(8,128)} %fusion.6), kind=kOutput, calls=%fused_computation.9 | convolution fusion | flops 908623872 | bytes 4718592 | tf_op jit(solution)/shard_map/erf,erd->efd/dot_general | solution.py:67
  163.0 0.2 reduce-scatter.6.cloned.1.call-start
  163.2 0.8 copy-done.11
  164.0 4.2 %fusion = bf16[1,1536,768]{2,1,0:T(8,128)(2,1)} fusion(bf16[384,1536]{1,0:T(8,128)(2,1)} %bitcast.13, bf16[384,768]{1,0:T(8,128)(2,1)S(1)} %copy-done.11), kind=kOutput, calls=%fused_computation.8 | convolution fusion | flops 907149312 | bytes 4128768 | tf_op jit(solution)/shard_map/erd,erf->edf/dot_general | solution.py:66
  168.3 3.5 %reshape.179 = bf16[4,128,12,128]{1,0,3,2:T(4,128)(2,1)} reshape(bf16[1,512,1536]{1,2,0:T(8,128)(2,1)} %all-gather.6.cloned.1.call-done) | data formatting | bytes 3145728 | tf_op jit(solution)/shard_map/while/body/eval_jaxpr/reshape | solution.py:143
  171.8 3.4 %fusion.3 = bf16[12,512,128]{2,1,0:T(8,128)(2,1)} fusion(f32[12,512,128]{2,1,0:T(8,128)} %get-tuple-element.67, f32[12,512]{1,0:T(8,128)S(1)} %copy-done.8), kind=kLoop, calls=%fused_computation.13 | loop fusion | flops 2359296 | bytes 4743168 | tf_op jit(solution)/shard_map/while/body/eval_jaxpr/convert_element_type | solution.py:132
  175.2 4.0 %reshape.185 = bf16[4,128,12,128]{3,2,1,0:T(8,128)(2,1)} reshape(bf16[512,1536]{1,0:T(8,128)(2,1)} %all-gather.4.cloned.1.call-done) | data formatting | bytes 3145728 | tf_op jit(solution)/shard_map/while/body/eval_jaxpr/reshape | solution.py:144
  179.2 3.9 %fusion.14 = bf16[4,128,12,128]{1,3,2,0:T(8,128)(2,1)} fusion(bf16[12,4,128,128]{3,2,1,0:T(8,128)(2,1)} %bitcast.88, bf16[4,128,12,128]{3,2,1,0:T(8,128)(2,1)} %reshape.185), kind=kOutput, calls=%fused_computation.26 | convolution fusion | flops 202113024 | bytes 4718592 | tf_op jit(solution)/shard_map/while/body/eval_jaxpr/hgqk,gqhd->gkhd/dot_general | solution.py:151
  183.1 1.7 reduce_sum.81
  184.8 0.9 copy.94
  185.7 4.3 %fusion.19 = bf16[4,128,12,128]{3,1,2,0:T(8,128)(2,1)} fusion(bf16[4,128,12,128]{1,0,3,2:T(4,128)(2,1)} %reshape.179, bf16[12,4,128,128]{3,2,1,0:T(8,128)(2,1)} %bitcast.84), kind=kOutput, calls=%fused_computation.27 | convolution fusion | flops 202899456 | bytes 4718592 | tf_op jit(solution)/shard_map/while/body/eval_jaxpr/hgqk,gqhd->gkhd/dot_general | solution.py:146
  190.0 1.7 reduce_sum.80
  191.7 0.2 copy.88
  192.0 0.9 copy.93
  192.9 1.2 copy.105
  194.1 0.9 copy.92
  195.1 25.8 %reduce-scatter.8.cloned.1.call-done = bf16[1,192,1536]{2,1,0:T(8,128)(2,1)} async-done(((bf16[1,768,1536]{2,1,0:T(8,128)(2,1)}), bf16[1,192,1536]{2,1,0:T(8,128)(2,1)}) %reduce-scatter.8.cloned.1.call-update) | async-done | bytes 589840 | tf_op jit(solution)/shard_map/reduce_scatter | solution.py:80
  220.9 35.8 %reduce-scatter.6.cloned.1.call-done = bf16[1,384,768]{2,1,0:T(8,128)(2,1)} async-done(((bf16[1,1536,768]{2,1,0:T(8,128)(2,1)}), bf16[1,384,768]{2,1,0:T(8,128)(2,1)}) %reduce-scatter.6.cloned.1.call-update) | async-done | bytes 589840 | tf_op jit(solution)/shard_map/reduce_scatter | solution.py:77
  (50 shorter events, 1.4 us)
Async XLA Ops:
  7.2 44.8 %copy-start = (bf16[1,1536,768]{2,1,0:T(8,128)(2,1)S(1)}, bf16[1,1536,768]{2,1,0:T(8,128)(2,1)}, u32[]{:S(2)}) copy-start(bf16[1,1536,768]{2,1,0:T(8,128)(2,1)} %param.16) | copy-start | bytes 7077892
  9.7 10.4 %copy-start.2 = (bf16[384,128]{1,0:T(8,128)(2,1)}, bf16[384,128]{1,0:T(8,128)(2,1)S(1)}, u32[]{:S(2)}) copy-start(bf16[384,128]{1,0:T(8,128)(2,1)S(1)} %convert_reduce_fusion) | copy-start | bytes 294916
  12.2 7.4 %copy-start.9 = (f32[1,128,2]{1,2,0:T(2,128)S(1)}, f32[1,128,2]{1,2,0:T(2,128)}, u32[]{:S(2)}) copy-start(f32[1,128,2]{1,2,0:T(2,128)} %param.15) | copy-start | bytes 3076
  12.2 7.9 %copy-start.3 = (bf16[1,128,1536]{2,1,0:T(8,128)(2,1)S(1)}, bf16[1,128,1536]{2,1,0:T(8,128)(2,1)}, u32[]{:S(2)}) copy-start(bf16[1,128,1536]{2,1,0:T(8,128)(2,1)} %param.13) | copy-start | bytes 1179652
  12.2 36.1 %all-to-all-start.1 = ((bf16[8,48,1536]{2,1,0:T(8,128)(2,1)}), bf16[8,48,1536]{2,1,0:T(8,128)(2,1)}, u32[]{:S(2)}, u32[]{:S(2)}) async-start(bf16[8,48,1536]{2,1,0:T(8,128)(2,1)} %bitcast.12), calls=%async_computation.1 | async-start | bytes 2359296 | tf_op jit(solution)/shard_map/all_to_all | solution.py:45
  48.3 32.4 %all-to-all-start = ((bf16[8,48,1536]{2,1,0:T(8,128)(2,1)}), bf16[8,48,1536]{2,1,0:T(8,128)(2,1)S(1)}, u32[]{:S(2)}, u32[]{:S(2)}) async-start(bf16[8,48,1536]{2,1,0:T(8,128)(2,1)} %bitcast.8), calls=%async_computation | async-start | bytes 2359296 | tf_op jit(solution)/shard_map/all_to_all | solution.py:46
  80.7 3.6 %copy-start.5 = (bf16[8,48,1536]{2,1,0:T(8,128)(2,1)}, bf16[8,48,1536]{2,1,0:T(8,128)(2,1)S(1)}, u32[]{:S(2)}) copy-start(bf16[8,48,1536]{2,1,0:T(8,128)(2,1)S(1)} %all-to-all-done) | copy-start | bytes 3538948
  84.4 2.3 copy-start.10
  86.6 32.4 %all-to-all-start.2 = ((bf16[8,48,1536]{2,1,0:T(8,128)(2,1)}), bf16[8,48,1536]{2,1,0:T(8,128)(2,1)S(1)}, u32[]{:S(2)}, u32[]{:S(2)}) async-start(bf16[8,48,1536]{2,1,0:T(8,128)(2,1)} %bitcast.99), calls=%async_computation.2 | async-start | bytes 2359296 | tf_op jit(solution)/shard_map/all_to_all | solution.py:71
  90.3 34.6 %all-gather.6.cloned.1.call-start = ((), (), s32[]{:S(2)}) async-start(), calls=%async_computation.9 | async-start | bytes 1966080 | tf_op jit(solution)/shard_map/all_gather | solution.py:98
  92.3 50.6 %all-gather.4.cloned.1.call-start = ((), (), s32[]{:S(2)}) async-start(), calls=%async_computation.6 | async-start | bytes 1966080 | tf_op jit(solution)/shard_map/all_gather | solution.py:99
  121.7 71.2 %reduce-scatter.10.cloned.1.call-start = ((), (), s32[]{:S(2)}) async-start(), calls=%async_computation.10 | async-start | bytes 1966080
  142.8 2.7 %copy-start.7 = (f32[12,512]{1,0:T(8,128)}, f32[12,512]{1,0:T(8,128)S(1)}, u32[]{:S(2)}) copy-start(f32[12,512]{1,0:T(8,128)S(1)} %log_bitcast_fusion) | copy-start | bytes 73732
  142.8 2.7 %copy-start.4 = (bf16[1,128,1536]{1,2,0:T(8,128)(2,1)S(1)}, bf16[1,128,1536]{1,2,0:T(8,128)(2,1)}, u32[]{:S(2)}) copy-start(bf16[1,128,1536]{1,2,0:T(8,128)(2,1)} %copy.80) | copy-start | bytes 1179652
  149.4 1.2 copy-start.1
  157.5 1.3 copy-start.6
  157.6 63.3 %reduce-scatter.8.cloned.1.call-start = ((), (), s32[]{:S(2)}) async-start(), calls=%async_computation.8 | async-start | bytes 2949120 | tf_op jit(solution)/shard_map/reduce_scatter | solution.py:80
  163.0 1.1 copy-start.11
  163.0 93.7 %reduce-scatter.6.cloned.1.call-start = ((), (), s32[]{:S(2)}) async-start(), calls=%async_computation.7 | async-start | bytes 2949120 | tf_op jit(solution)/shard_map/reduce_scatter | solution.py:77
  168.3 3.5 %copy-start.8 = (f32[12,512]{1,0:T(8,128)S(1)}, f32[12,512]{1,0:T(8,128)}, u32[]{:S(2)}) copy-start(f32[12,512]{1,0:T(8,128)} %copy-done.7) | copy-start | bytes 73732
Sparse Core Ops, SparseCore 0:
  93.2 21.1 all-gather.5
  121.8 18.9 all-gather.3
  157.7 27.3 reduce-scatter.9
  188.0 32.8 reduce-scatter.7
  223.9 32.8 reduce-scatter.5
where the time goes:
time: 264 us; the launch traced here: 263 us
  waiting for transfers between devices  141 us (53%)
  matrix products  41.9 us (16%)
  local copies, waits for them, and re-layouts  31.9 us (12%)
  starting transfers between devices  15.1 us (6%)
  between operations  14 us (5%)
  blocking collectives  11.3 us (4%)
  other arithmetic  8.42 us (3%)
    reduce_scatter x1, waiting for transfers between devices, per_device(): lax.psum_scatter(first_term.astype(jnp.bfloat16), 'ctx', scatter_dimensio...  35.8 us
    all_to_all x1, waiting for transfers between devices, per_device(): lax.all_to_all(sent_rows.reshape(shape), 'exp', split_axis=0, concat_axis...  26.8 us
    all_to_all x1, waiting for transfers between devices, per_device(): lax.all_to_all(back_send, 'exp', split_axis=0, concat_axis=0, tiled=True)  26.7 us
    reduce_scatter x1, waiting for transfers between devices, per_device(): lax.psum_scatter(second_term.astype(jnp.bfloat16), 'ctx', scatter_dimensi...  25.8 us
    all_to_all x1, waiting for transfers between devices, per_device(): lax.all_to_all(sent_grads.reshape(shape), 'exp', split_axis=0, concat_axi...  25.4 us
    unnamed x34, local copies, waits for them, and re-layouts  16 us
    psum x1, blocking collectives, per_device(): lax.psum(own_delta.astype(jnp.bfloat16), 'ctx').astype(jnp.float32)  11.3 us
    all_to_all x1, starting transfers between devices, per_device(): lax.all_to_all(sent_rows.reshape(shape), 'exp', split_axis=0, concat_axis...  7.44 us
  transfers between devices with their start and end apart: 8, of which 5 were waited for; matrix products, arithmetic and copies ran while one was open for 21% of the time, Pallas kernels for 0%

commit v1 on v0

--- a/solution.py
+++ b/solution.py
@@ -1,6 +1,8 @@
 import jax
 import jax.numpy as jnp
 from jax import lax
+from jax.experimental import pallas as pl
+from jax.experimental.pallas import tpu as pltpu
 from jax.sharding import PartitionSpec as P
 
 HEAD_DIM = 128
@@ -11,7 +13,7 @@
     return lax.optimization_barrier(x.astype(jnp.bfloat16)).astype(jnp.float32)
 
 
-def per_device(
+def general(
     queries, key_states, value_states, attended, output_grad, expert_ids, gate_weights, w_in, w_out
 ):
     tok = queries.shape[1]
@@ -170,6 +172,512 @@
     return (query_sum[None], key_grad[None], value_grad[None], w_in_grad, w_out_grad)
 
 
+F32, BF16 = jnp.float32, jnp.bfloat16
+NT = (((1,), (1,)), ((), ()))
+TN = (((0,), (0,)), ((), ()))
+WIDE = 512
+EXPERTS = 8
+SOON, LATER = (2, 3, 6), (0, 1, 7, 4, 5)
+FIRST, LAST = (0, 1, 2, 3, 6), (7, 4, 5)
+
+
+GROUPS = ((0, 2), (2, 3))
+
+
+def grant(mebibytes):
+    return pltpu.CompilerParams(vmem_limit_bytes=mebibytes << 20)
+
+
+def vmem_specs(count):
+    return [pl.BlockSpec(memory_space=pltpu.VMEM)] * count
+
+
+def fill_payloads(partners, pick_ref, gate_ref, rows_ref, grads_ref, out_refs, capacity):
+    spans = [slice(p * capacity, (p + 1) * capacity) for p in partners]
+    pick = jnp.concatenate([pick_ref[span, :] for span in spans], axis=0)
+    gate = jnp.concatenate([gate_ref[span, :] for span in spans], axis=0)
+    for n in range(0, rows_ref.shape[1], WIDE):
+        cols = slice(n, n + WIDE)
+        rows = jnp.dot(pick, rows_ref[:, cols], preferred_element_type=F32).astype(BF16)
+        grads = jnp.dot(pick, grads_ref[:, cols], preferred_element_type=F32) * gate
+        grads = grads.astype(BF16)
+        place = 0
+        for b, p in enumerate(partners):
+            span = slice(b * capacity, (b + 1) * capacity)
+            if p in LAST:
+                out_refs[place][:, cols] = rows[span]
+                out_refs[place + 1][:, cols] = grads[span]
+                place += 2
+            else:
+                out_refs[place][:capacity, cols] = rows[span]
+                out_refs[place][capacity:, cols] = grads[span]
+                place += 1
+
+
+def payload_shapes(partners, capacity, width):
+    one = jax.ShapeDtypeStruct((2 * capacity, width), BF16)
+    part = jax.ShapeDtypeStruct((capacity, width), BF16)
+    return tuple(x for p in partners for x in ((part, part) if p in LAST else (one,)))
+
+
+def pick_slots(ids, gates, rows, grads, capacity):
+    tok, width = rows.shape
+    payloads = payload_shapes(SOON, capacity, width)
+    given = (ids, gates, rows, grads)
+
+    def kernel(*refs):
+        pick_ref, gate_ref = refs[4:6]
+        out_refs = refs[6 : 6 + len(payloads)]
+        ids_ref, gates_ref, rows_ref, grads_ref = held = refs[-8:-4]
+        copies = [pltpu.make_async_copy(a, b, s) for a, b, s in zip(refs[:4], held, refs[-4:])]
+        for copy in copies:
+            copy.start()
+        copies[0].wait()
+        copies[1].wait()
+        me = lax.axis_index("exp")
+        first, second = ids_ref[0:1, :] ^ me, ids_ref[1:2, :] ^ me
+        expert = lax.broadcasted_iota(jnp.int32, (EXPERTS, tok), 0)
+        is_first, is_second = first == expert, second == expert
+        member = jnp.where(is_first | is_second, 1.0, 0.0)
+        earlier = jnp.where(
+            lax.broadcasted_iota(jnp.int32, (tok, tok), 0)
+            < lax.broadcasted_iota(jnp.int32, (tok, tok), 1),
+            1.0,
+            0.0,
+        )
+        before = jnp.dot(member.astype(BF16), earlier.astype(BF16), preferred_element_type=F32)
+        slot = jnp.where(member > 0, before, -1.0).astype(jnp.int32)
+        gate = jnp.where(is_first, gates_ref[0:1, :], 0.0) + jnp.where(
+            is_second, gates_ref[1:2, :], 0.0
+        )
+        place = lax.broadcasted_iota(jnp.int32, (capacity, tok), 0)
+        for e in range(EXPERTS):
+            chosen = jnp.where(slot[e : e + 1, :] == place, 1.0, 0.0)
+            span = slice(e * capacity, (e + 1) * capacity)
+            pick_ref[span, :] = chosen.astype(BF16)
+            gate_ref[span, :] = jnp.sum(chosen * gate[e : e + 1, :], axis=1, keepdims=True)
+        copies[2].wait()
+        copies[3].wait()
+        fill_payloads(SOON, pick_ref, gate_ref, rows_ref, grads_ref, out_refs, capacity)
+
+    return pl.pallas_call(
+        kernel,
+        out_shape=(
+            jax.ShapeDtypeStruct((EXPERTS * capacity, tok), BF16),
+            jax.ShapeDtypeStruct((EXPERTS * capacity, 1), F32),
+        )
+        + payloads,
+        in_specs=[pl.BlockSpec(memory_space=pltpu.HBM)] * 4,
+        out_specs=tuple(vmem_specs(2 + len(payloads))),
+        scratch_shapes=[pltpu.VMEM(x.shape, x.dtype) for x in given]
+        + [pltpu.SemaphoreType.DMA] * 4,
+        compiler_params=grant(20),
+        name="pick_slots",
+    )(*given)
+
+
+def pick_rest(pick, gate, rows, grads, capacity):
+    payloads = payload_shapes(LATER, capacity, rows.shape[1])
+
+    def kernel(pick_ref, gate_ref, rows_ref, grads_ref, *out_refs):
+        fill_payloads(LATER, pick_ref, gate_ref, rows_ref, grads_ref, out_refs, capacity)
+
+    return pl.pallas_call(
+        kernel,
+        out_shape=payloads,
+        in_specs=vmem_specs(4),
+        out_specs=tuple(vmem_specs(len(payloads))),
+        compiler_params=grant(20),
+        name="pick_rest",
+    )(pick, gate, rows, grads)
+
+
+def upper_only(rows, w_first):
+    capacity, width = rows[0].shape
+    slots, hidden = len(rows) * capacity, w_first.shape[1]
+    tile = 256
+
+    def kernel(*refs):
+        first_ref, upper_ref, act_ref = refs[len(rows) :]
+        held = jnp.concatenate([r[...] for r in refs[: len(rows)]], axis=0)
+        upper = jnp.dot(held, first_ref[...], preferred_element_type=F32)
+        upper_ref[...] = upper
+        act_ref[...] = (upper * jax.nn.sigmoid(upper)).astype(BF16)
+
+    return pl.pallas_call(
+        kernel,
+        grid=(hidden // tile,),
+        out_shape=(
+            jax.ShapeDtypeStruct((slots, hidden), F32),
+            jax.ShapeDtypeStruct((slots, hidden), BF16),
+        ),
+        in_specs=[pl.BlockSpec((capacity, width), lambda f: (0, 0))] * len(rows)
+        + [pl.BlockSpec((width, tile), lambda f: (0, f))],
+        out_specs=(pl.BlockSpec((slots, tile), lambda f: (0, f)),) * 2,
+        compiler_params=grant(20),
+        name="upper_only",
+    )(*rows, w_first)
+
+
+def run_experts(rows, grads, upper, w_first, w_second):
+    count, (width, hidden) = len(grads), w_first.shape
+    capacity = grads[0][0].shape[0] - grads[0][1]
+    slots = count * capacity
+    tile = 256
+    arrays = [a for a, _ in grads]
+    extra = [] if upper is None else [upper]
+
+    def kernel(*refs):
+        ins = refs[:count]
+        first_ref, second_ref = refs[count : count + 2]
+        outs = refs[count + 2 + len(extra) :]
+        total_ref = outs[-1]
+        cotangents = jnp.concatenate(
+            [r[low : low + capacity, :] for r, (_, low) in zip(ins, grads)], axis=0
+        )
+        if extra:
+            upper, (up_ref, *back_refs) = refs[count + 2][...], outs[:-1]
+        else:
+            act_ref, up_ref, *back_refs = outs[:-1]
+            held = jnp.concatenate(
+                [r[low : low + capacity, :] for r, (_, low) in zip(ins, rows)], axis=0
+            )
+            upper = jnp.dot(held, first_ref[...], preferred_element_type=F32)
+        act_grad = lax.dot_general(cotangents, second_ref[...], NT, preferred_element_type=F32)
+        sig = jax.nn.sigmoid(upper)
+        if not extra:
+            act_ref[...] = (upper * sig).astype(BF16)
+        up = (act_grad * sig * (1.0 + upper * (1.0 - sig))).astype(BF16)
+        up_ref[...] = up
+        back = lax.dot_general(up, first_ref[...], NT, preferred_element_type=F32)
+        step, last = pl.program_id(0), hidden // tile - 1
+
+        @pl.when(step == 0)
+        def _():
+            total_ref[...] = back
+
+        @pl.when((step > 0) & (step < last))
+        def _():
+            total_ref[...] += back
+
+        @pl.when(step == last)
+        def _():
+            total = (total_ref[...] + back).astype(BF16)
+            for b, ref in enumerate(back_refs):
+                ref[...] = total[b * capacity : (b + 1) * capacity]
+
+    narrow = pl.BlockSpec((slots, tile), lambda f: (0, f))
+    hidden_outs = 1 if extra else 2
+    outs = pl.pallas_call(
+        kernel,
+        grid=(hidden // tile,),
+        out_shape=(jax.ShapeDtypeStruct((slots, hidden), BF16),) * hidden_outs
+        + (jax.ShapeDtypeStruct((capacity, width), BF16),) * count,
+        in_specs=[pl.BlockSpec(a.shape, lambda f: (0, 0)) for a in arrays]
+        + [
+            pl.BlockSpec((width, tile), lambda f: (0, f)),
+            pl.BlockSpec((tile, width), lambda f: (f, 0)),
+        ]
+        + [narrow] * len(extra),
+        out_specs=(narrow,) * hidden_outs
+        + (pl.BlockSpec((capacity, width), lambda f: (0, 0)),) * count,
+        scratch_shapes=[pltpu.VMEM((slots, width), F32)],
+        compiler_params=grant(20),
+        name="run_experts",
+    )(*arrays, w_first, w_second, *extra)
+    return (*outs[:hidden_outs], outs[hidden_outs:])
+
+
+def weight_terms(left, right, capacity, places, pieces):
+    rows, cols = left[0][0].shape[1], right[0][0].shape[1]
+    share = rows // 4
+    size = share // pieces
+    outs = len(places) * pieces
+    count = len(left)
+
+    def gather(refs, parts):
+        return jnp.concatenate(
+            [
+                r[...] if low is None else r[low : low + capacity, :]
+                for r, (_, low) in zip(refs, parts)
+            ],
+            axis=0,
+        )
+
+    def kernel(*refs):
+        turned_ref = refs[-1]
+        turned_ref[...] = gather(refs[:count], left).T
+        held = gather(refs[count:], right)
+        out_refs = refs[count + len(right) : -1]
+        me = lax.axis_index("ctx")
+        for n in range(outs):
+            begin = (me ^ places[n // pieces]) * share + n % pieces * size
+            rows_here = pl.ds(pl.multiple_of(begin, size), size)
+            out_refs[n][...] = jnp.dot(
+                turned_ref[rows_here, :], held, preferred_element_type=F32
+            ).astype(BF16)
+
+    slots = sum(a.shape[0] if low is None else capacity for a, low in left)
+    return pl.pallas_call(
+        kernel,
+        out_shape=(jax.ShapeDtypeStruct((size, cols), BF16),) * outs,
+        in_specs=vmem_specs(count + len(right)),
+        out_specs=tuple(vmem_specs(outs)),
+        scratch_shapes=[pltpu.VMEM((rows, slots), BF16)],
+        compiler_params=grant(20),
+        name="weight_terms",
+    )(*[a for a, _ in left], *[a for a, _ in right])
+
+
+def add_back(pick, returned, grads, column, size):
+    tok = grads.shape[0]
+    capacity = returned[0].shape[0]
+
+    def kernel(pick_ref, grads_ref, *refs):
+        back = jnp.concatenate([r[...] for r in refs[:-1]], axis=0)
+        total = lax.dot_general(pick_ref[...], back, TN, preferred_element_type=F32)
+        refs[-1][...] = (grads_ref[...].astype(F32) + total).astype(BF16)
+
+    return pl.pallas_call(
+        kernel,
+        grid=(1,),
+        out_shape=jax.ShapeDtypeStruct((tok, size), BF16),
+        in_specs=[pl.BlockSpec(pick.shape, lambda i: (0, 0))]
+        + [pl.BlockSpec((tok, size), lambda i: (0, column // size))]
+        + [pl.BlockSpec((capacity, size), lambda i: (0, column // size))] * len(returned),
+        out_specs=pl.BlockSpec((tok, size), lambda i: (0, 0)),
+        compiler_params=grant(20),
+        name="add_back",
+    )(pick, grads, *returned)
+
+
+def head_specs(count, tok, step, first=0):
+    return [pl.BlockSpec((tok, step * HEAD_DIM), lambda h: (0, h + first // step))] * count
+
+
+def stacked(refs, cols):
+    return jnp.concatenate([r[:, cols] for r in refs], axis=0)
+
+
+def with_delta(grads, attended):
+    product = grads.astype(F32) * attended.astype(F32)
+    return jnp.concatenate([grads, product.astype(BF16)], axis=1)
+
+
+def with_ones(values):
+    return jnp.concatenate([values, jnp.full_like(values, -1.0)], axis=1)
+
+
+def probabilities(query_blocks, key_blocks):
+    tok, width = query_blocks[0].shape
+    heads, count = width // HEAD_DIM, len(query_blocks)
+    total = count * tok
+    scale = HEAD_DIM**-0.5
+    step = 2
+
+    def kernel(*refs):
+        by_query_ref, by_key_ref = refs[2 * count :]
+        for h in range(step):
+            cols = slice(h * HEAD_DIM, (h + 1) * HEAD_DIM)
+            q, k = stacked(refs[:count], cols), stacked(refs[count : 2 * count], cols)
+            row = jnp.exp(lax.dot_general(q[:tok], k, NT, preferred_element_type=F32) * scale)
+            by_query_ref[h] = (row / jnp.sum(row, axis=1, keepdims=True)).astype(BF16)
+            col = jnp.exp(lax.dot_general(k[:tok], q, NT, preferred_element_type=F32) * scale)
+            norm = jnp.sum(col, axis=0, keepdims=True)
+            for b in range(1, count):
+                other = lax.dot_general(
+                    k[b * tok : (b + 1) * tok], q, NT, preferred_element_type=F32
+                )
+                norm = norm + jnp.sum(jnp.exp(other * scale), axis=0, keepdims=True)
+            by_key_ref[h] = (col / norm).astype(BF16)
+
+    shape = jax.ShapeDtypeStruct((heads, tok, total), BF16)
+    return pl.pallas_call(
+        kernel,
+        grid=(heads // step,),
+        out_shape=(shape, shape),
+        in_specs=head_specs(2 * count, tok, step),
+        out_specs=(pl.BlockSpec((step, tok, total), lambda h: (h, 0, 0)),) * 2,
+        compiler_params=grant(20),
+        name="probabilities",
+    )(*query_blocks, *key_blocks)
+
+
+def query_side(span, g, attended, probs, key_blocks, value_blocks, before):
+    first, last = span
+    tok, width = attended.shape
+    count, step = len(key_blocks), 4
+    scale = HEAD_DIM**-0.5
+    carried = [] if before is None else [before]
+
+    def kernel(*refs):
+        g_ref, att_ref, probs_ref = refs[:3]
+        out_ref = refs[-1]
+        for h in range(step):
+            cols = slice(h * HEAD_DIM, (h + 1) * HEAD_DIM)
+            keys = stacked(refs[3 : 3 + count], cols)
+            values = with_ones(stacked(refs[3 + count : 3 + 2 * count], cols))
+            both = with_delta(g_ref[:, cols], att_ref[:, cols])
+            diff = lax.dot_general(both, values, NT, preferred_element_type=F32)
+            score = (probs_ref[h].astype(F32) * diff).astype(BF16)
+            grad = jnp.dot(score, keys, preferred_element_type=F32) * scale
+            out_ref[:, cols] = grad.astype(BF16)
+
+    return pl.pallas_call(
+        kernel,
+        grid=((last - first) // step,),
+        out_shape=jax.ShapeDtypeStruct((tok, width), BF16),
+        in_specs=head_specs(1, tok, step)
+        + head_specs(1, tok, step, first)
+        + [pl.BlockSpec((step, tok, count * tok), lambda h: (h + first // step, 0, 0))]
+        + head_specs(2 * count, tok, step, first)
+        + [pl.BlockSpec(memory_space=pl.ANY)] * len(carried),
+        out_specs=head_specs(1, tok, step, first)[0],
+        input_output_aliases={3 + 2 * count: 0} if carried else {},
+        compiler_params=grant(20),
+        name="query_side",
+    )(g, attended, probs, *key_blocks, *value_blocks, *carried)
+
+
+def key_side(span, g_blocks, attended_blocks, probs, query_blocks, values, before):
+    first, last = span
+    tok, width = values.shape
+    count, step = len(g_blocks), 4
+    scale = HEAD_DIM**-0.5
+    carried = [] if before is None else list(before)
+
+    def kernel(*refs):
+        probs_ref, v_ref = refs[:2]
+        key_ref, value_ref = refs[-2:]
+        for h in range(step):
+            cols = slice(h * HEAD_DIM, (h + 1) * HEAD_DIM)
+            g = stacked(refs[2 : 2 + count], cols)
+            both = with_delta(g, stacked(refs[2 + count : 2 + 2 * count], cols))
+            queries = stacked(refs[2 + 2 * count : 2 + 3 * count], cols)
+            diff = lax.dot_general(
+                with_ones(v_ref[:, cols]), both, NT, preferred_element_type=F32
+            )
+            probs = probs_ref[h]
+            score = (probs.astype(F32) * diff).astype(BF16)
+            grad = jnp.dot(score, queries, preferred_element_type=F32) * scale
+            key_ref[:, cols] = grad.astype(BF16)
+            value_ref[:, cols] = jnp.dot(probs, g, preferred_element_type=F32).astype(BF16)
+
+    shape = jax.ShapeDtypeStruct((tok, width), BF16)
+    return pl.pallas_call(
+        kernel,
+        grid=((last - first) // step,),
+        out_shape=(shape, shape),
+        in_specs=[pl.BlockSpec((step, tok, count * tok), lambda h: (h + first // step, 0, 0))]
+        + head_specs(1, tok, step, first)
+        + head_specs(count, tok, step)
+        + head_specs(2 * count, tok, step, first)
+        + [pl.BlockSpec(memory_space=pl.ANY)] * len(carried),
+        out_specs=tuple(head_specs(2, tok, step, first)),
+        input_output_aliases={2 + 3 * count: 0, 3 + 3 * count: 1} if carried else {},
+        compiler_params=grant(20),
+        name="key_side",
+    )(probs, values, *g_blocks, *attended_blocks, *query_blocks, *carried)
+
+
+def swap(values, axis, bits):
+    return lax.ppermute(values, axis, [(i, i ^ bits) for i in range(lax.axis_size(axis))])
+
+
+def stream_blocks(own):
+    across = swap(own, "ctx", 2)
+    return own, swap(own, "ctx", 1), across, swap(across, "ctx", 1)
+
+
+def across_chips(across, opposite):
+    opposite = swap(opposite, "ctx", 1)
+    sent = (across.astype(F32) + opposite.astype(F32)).astype(BF16)
+    return swap(sent, "ctx", 2)
+
+
+def total_rows(own, beside, others):
+    beside = swap(beside, "ctx", 1)
+    other = jnp.concatenate(others, axis=0).astype(F32)
+    return (own.astype(F32) + beside.astype(F32) + other).astype(BF16)[None]
+
+
+def trade(values, partner):
+    return swap(values, "exp", partner) if partner else values
+
+
+def quick(
+    queries, key_states, value_states, attended, output_grad, expert_ids, gate_weights, w_in, w_out
+):
+    tok, width = queries.shape[1:]
+    heads = width // HEAD_DIM
+    capacity = 3 * tok // EXPERTS
+    ids, gates = expert_ids[0].T, gate_weights[0].T
+    attn_rows, grad_rows = attended[0], output_grad[0]
+    inputs = (attn_rows, grad_rows, capacity)
+
+    pick, slot_gate, *soon = pick_slots(ids, gates, *inputs)
+    later = pick_rest(pick, slot_gate, *inputs)
+    sent = iter((*soon, *later))
+    rows, grads = {}, {}
+    for p in SOON + LATER:
+        if p in LAST:
+            rows[p] = (trade(next(sent), p), 0)
+            grads[p] = (trade(next(sent), p), 0)
+        else:
+            payload = trade(next(sent), p)
+            rows[p], grads[p] = (payload, 0), (payload, capacity)
+
+    query_blocks = stream_blocks(queries[0])
+    key_blocks = stream_blocks(key_states[0])
+    value_blocks = stream_blocks(value_states[0])
+    attended_blocks = stream_blocks(attn_rows)
+    by_query, by_key = probabilities(query_blocks, key_blocks)
+
+    weights = (w_in[0], w_out[0])
+    soon_rows, soon_grads = [rows[p] for p in FIRST], [grads[p] for p in FIRST]
+    late_rows, late_grads = [rows[p] for p in LAST], [grads[p] for p in LAST]
+    act_a, up_a, first = run_experts(soon_rows, soon_grads, None, *weights)
+    upper_b, act_b = upper_only([a for a, _ in late_rows], w_in[0])
+    up_b, last = run_experts([], late_grads, upper_b, *weights)
+    back = {p: trade(rows, p) for p, rows in zip(FIRST + LAST, (*first, *last))}
+    back = [back[p] for p in range(EXPERTS)]
+
+    out_terms = ([(act_a, None), (act_b, None)], soon_grads + late_grads, capacity)
+    in_terms = (soon_rows + late_rows, [(up_a, None), (up_b, None)], capacity)
+    out_3, out_2 = weight_terms(*out_terms, (3, 2), 1)
+    low_3, high_3, low_2, high_2 = weight_terms(*in_terms, (3, 2), 2)
+    out_1, out_0 = weight_terms(*out_terms, (1, 0), 1)
+    in_1, in_0 = weight_terms(*in_terms, (1, 0), 1)
+    out_other = across_chips(out_2, out_3)
+    low_other = across_chips(low_2, low_3)
+    high_other = across_chips(high_2, high_3)
+    w_out_grad = total_rows(out_0, out_1, [out_other])
+    w_in_grad = total_rows(in_0, in_1, [low_other, high_other])
+
+    query_grad = pair = None
+    for low, high in GROUPS:
+        span = (low * heads // 3, high * heads // 3)
+        column, size = low * width // 3, (high - low) * width // 3
+        g = add_back(pick, back, grad_rows, column, size)
+        g_blocks = stream_blocks(g)
+        query_grad = query_side(span, g, attn_rows, by_query, key_blocks, value_blocks, query_grad)
+        pair = key_side(
+            span, g_blocks, attended_blocks, by_key, query_blocks,
+            value_states[0], pair,
+        )
+    key_grad, value_grad = pair
+    return (query_grad[None], key_grad[None], value_grad[None], w_in_grad, w_out_grad)
+
+
+def per_device(queries, *rest):
+    tok, width = queries.shape[1:]
+    fits = lax.axis_size("ctx") == 4 and lax.axis_size("exp") == EXPERTS
+    fits = fits and tok % 128 == 0 and (3 * tok // EXPERTS) % 16 == 0
+    if fits and width % (12 * HEAD_DIM) == 0 and rest[-1].shape[1] % 256 == 0:
+        return quick(queries, *rest)
+    return general(queries, *rest)
+
+
 def solution(mesh):
     return jax.shard_map(
         per_device,

time: 264 us -> 158 us (0.60)
  waiting for transfers between devices: 141 us -> 65.6 us
  matrix products: 41.9 us -> 0 us
  starting transfers between devices: 15.1 us -> 52.7 us
  Pallas kernels: 0 us -> 28.3 us
  local copies, waits for them, and re-layouts: 31.9 us -> 7.55 us
  between operations: 14 us -> 0.87 us
  blocking collectives: 11.3 us -> 0 us
  other arithmetic: 8.42 us -> 2.4 us
    all_to_all x3 -> x0, waiting for transfers between devices: 78.9 us -> none  [the longest x1 26.8 us: per_device(): lax.all_to_all(sent_rows.reshape(shape), 'exp', split_axis=0, concat_axis...]
    ppermute x0 -> x43, waiting for transfers between devices: none -> 65.6 us  [swap(): lax.ppermute(values, axis, [(i, i ^ bits) for i in range(lax.axis_size(ax...]
    reduce_scatter x2 -> x0, waiting for transfers between devices: 61.6 us -> none  [the longest x1 35.8 us: per_device(): lax.psum_scatter(first_term.astype(jnp.bfloat16), 'ctx', scatter_dimensio...]
    ppermute x0 -> x43, starting transfers between devices: none -> 52.7 us  [swap(): lax.ppermute(values, axis, [(i, i ^ bits) for i in range(lax.axis_size(ax...]
    dot_general x13 -> x0, matrix products: 41.9 us -> none  [the longest x1 4.3 us: grad_step(): jnp.einsum('hgqk,gqhd->gkhd', split_grad, split_query, preferred_element_...]
    pallas_call x0 -> x16, Pallas kernels: none -> 28.3 us  [the longest x2 6.9 us: run_experts(): pl.pallas_call(kernel, grid=(hidden // tile,), out_shape=(jax.ShapeDtypeS...]
    all_to_all x3 -> x0, starting transfers between devices: 14.7 us -> none  [the longest x1 7.44 us: per_device(): lax.all_to_all(sent_rows.reshape(shape), 'exp', split_axis=0, concat_axis...]
    psum x1 -> x0, blocking collectives: 11.3 us -> none  [per_device(): lax.psum(own_delta.astype(jnp.bfloat16), 'ctx').astype(jnp.float32)]
  transfers between devices with their start and end apart: 8 -> 43, of which waited for: 5 -> 17; matrix products, arithmetic and copies ran while one was open for 21% -> 1% of each run, Pallas kernels for 0% -> 17%
where the time goes in v1:
time: 158 us; the launch traced here: 157 us
  waiting for transfers between devices  65.6 us (42%)
  starting transfers between devices  52.7 us (33%)
  Pallas kernels  28.3 us (18%)
  local copies, waits for them, and re-layouts  7.55 us (5%)
  other arithmetic  2.4 us (2%)
    ppermute x43, waiting for transfers between devices, swap(): lax.ppermute(values, axis, [(i, i ^ bits) for i in range(lax.axis_size(ax...  65.6 us
    ppermute x43, starting transfers between devices, swap(): lax.ppermute(values, axis, [(i, i ^ bits) for i in range(lax.axis_size(ax...  52.7 us
    unnamed x28, local copies, waits for them, and re-layouts  7.55 us
    pallas_call x2, Pallas kernels, run_experts(): pl.pallas_call(kernel, grid=(hidden // tile,), out_shape=(jax.ShapeDtypeS...  6.9 us
    pallas_call x2, Pallas kernels, key_side(): pl.pallas_call(kernel, grid=((last - first) // step,), out_shape=(shape,...  5.15 us
    pallas_call x2, Pallas kernels, query_side(): pl.pallas_call(kernel, grid=((last - first) // step,), out_shape=jax.Shap...  4.59 us
    pallas_call x1, Pallas kernels, probabilities(): pl.pallas_call(kernel, grid=(heads // step,), out_shape=(shape, shape), i...  4.33 us
    pallas_call x4, Pallas kernels, weight_terms(): pl.pallas_call(kernel, out_shape=(jax.ShapeDtypeStruct((size, cols), BF16...  4.08 us
  transfers between devices with their start and end apart: 43, of which 17 were waited for; matrix products, arithmetic and copies ran while one was open for 1% of the time, Pallas kernels for 17%

profile of v1, /device:TPU:0, one launch (start us, length us, event | category | flops | bytes accessed | tf_op | source)
XLA Modules:
  0.0 157.4 jit_solution(2834782144613244011)
XLA Ops:
  1.6 1.0 copy-done.7
  4.0 1.1 pick_slots.1
  6.1 1.0 copy-done.8
  7.6 6.1 %collective-permute-start.10 = (bf16[48,1536]{1,0:T(8,128)(2,1)S(1)}, bf16[48,1536]{1,0:T(8,128)(2,1)S(1)}, u32[]{:S(2)}, u32[]{:S(2)}) collective-permute-start(bf16[48,1536]{1,0:T(8,128)(2,1)S(1)} %get-tuple-element.61), channel_id=1, source_target_pairs={{0,7},{1,6},{2,5},{3,4},{4,3},{5,2},{6,1},{7,0},{8,15},{9,14},{10,... | collective-permute-start | bytes 442376 | tf_op jit(solution)/shard_map/ppermute | solution.py:584
  13.7 2.9 %collective-permute-start.12 = (bf16[48,1536]{1,0:T(8,128)(2,1)S(1)}, bf16[48,1536]{1,0:T(8,128)(2,1)S(1)}, u32[]{:S(2)}, u32[]{:S(2)}) collective-permute-start(bf16[48,1536]{1,0:T(8,128)(2,1)S(1)} %get-tuple-element.63), channel_id=1, source_target_pairs={{0,5},{1,4},{2,7},{3,6},{4,1},{5,0},{6,3},{7,2},{8,13},{9,12},{10,... | collective-permute-start | bytes 442376 | tf_op jit(solution)/shard_map/ppermute | solution.py:584
  16.6 1.2 collective-permute-start.7
  18.5 1.6 %collective-permute-start = (bf16[96,1536]{1,0:T(8,128)(2,1)S(1)}, bf16[96,1536]{1,0:T(8,128)(2,1)S(1)}, u32[]{:S(2)}, u32[]{:S(2)}) collective-permute-start(bf16[96,1536]{1,0:T(8,128)(2,1)S(1)} %get-tuple-element.50), channel_id=1, source_target_pairs={{0,1},{1,0},{2,3},{3,2},{4,5},{5,4},{6,7},{7,6},{8,9},{9,8},{10,11... | collective-permute-start | bytes 884744 | tf_op jit(solution)/shard_map/ppermute | solution.py:584
  20.1 16.4 %collective-permute-done.11.refs_1_.refs_6_ = bf16[48,1536]{1,0:T(8,128)(2,1)S(1)} collective-permute-done((bf16[48,1536]{1,0:T(8,128)(2,1)S(1)}, bf16[48,1536]{1,0:T(8,128)(2,1)S(1)}, u32[]{:S(2)}, u32[]{:S(2)}) %collective-permute-start.11) | collective-permute-done | bytes 147488 | tf_op jit(solution)/shard_map/ppermute | solution.py:584
  36.6 4.7 %collective-permute-done.12.refs_2_.refs_7_ = bf16[48,1536]{1,0:T(8,128)(2,1)S(1)} collective-permute-done((bf16[48,1536]{1,0:T(8,128)(2,1)S(1)}, bf16[48,1536]{1,0:T(8,128)(2,1)S(1)}, u32[]{:S(2)}, u32[]{:S(2)}) %collective-permute-start.12) | collective-permute-done | bytes 147488 | tf_op jit(solution)/shard_map/ppermute | solution.py:584
  41.3 1.4 collective-permute-start.1
  42.8 4.7 %collective-permute-start.2 = (bf16[96,1536]{1,0:T(8,128)(2,1)S(1)}, bf16[96,1536]{1,0:T(8,128)(2,1)S(1)}, u32[]{:S(2)}, u32[]{:S(2)}) collective-permute-start(bf16[96,1536]{1,0:T(8,128)(2,1)S(1)} %get-tuple-element.52), channel_id=1, source_target_pairs={{0,3},{1,2},{2,1},{3,0},{4,7},{5,6},{6,5},{7,4},{8,11},{9,10},{10,... | collective-permute-start | bytes 884744 | tf_op jit(solution)/shard_map/ppermute | solution.py:584
  47.5 1.8 %collective-permute-done.8.refs_1_.refs_8_ = bf16[48,1536]{1,0:T(8,128)(2,1)S(1)} collective-permute-done((bf16[48,1536]{1,0:T(8,128)(2,1)S(1)}, bf16[48,1536]{1,0:T(8,128)(2,1)S(1)}, u32[]{:S(2)}, u32[]{:S(2)}) %collective-permute-start.8) | collective-permute-done | bytes 147488 | tf_op jit(solution)/shard_map/ppermute | solution.py:584
  49.3 2.7 %collective-permute-start.3 = (bf16[96,1536]{1,0:T(8,128)(2,1)S(1)}, bf16[96,1536]{1,0:T(8,128)(2,1)S(1)}, u32[]{:S(2)}, u32[]{:S(2)}) collective-permute-start(bf16[96,1536]{1,0:T(8,128)(2,1)S(1)} %get-tuple-element.53), channel_id=1, source_target_pairs={{0,6},{1,7},{2,4},{3,5},{4,2},{5,3},{6,0},{7,1},{8,14},{9,15},{10,... | collective-permute-start | bytes 884744 | tf_op jit(solution)/shard_map/ppermute | solution.py:584
  52.4 1.5 collective-permute-start.18
  53.9 1.7 %copy-done = bf16[1,1536,768]{2,1,0:T(8,128)(2,1)S(1)} copy-done((bf16[1,1536,768]{2,1,0:T(8,128)(2,1)S(1)}, bf16[1,1536,768]{2,1,0:T(8,128)(2,1)}, u32[]{:S(2)}) %copy-start) | copy-done | bytes 2359320
  55.6 1.1 upper_only.1
  57.3 3.6 %run_experts.3 = (bf16[144,768]{1,0:T(8,128)(2,1)S(1)}, bf16[48,1536]{1,0:T(8,128)(2,1)S(1)}, bf16[48,1536]{1,0:T(8,128)(2,1)S(1)}, bf16[48,1536]{1,0:T(8,128)(2,1)S(1)}) custom-call(bf16[48,1536]{1,0:T(8,128)(2,1)S(1)} %collective-permute-done.7.refs_0_.refs_7_, bf16[48,1536]{1,0:T(8,128)(2,1)S(1)} %collective-permute-done.8.refs_1_.refs_8_, ...), custom_call_target="tpu_custom_call" | custom-call | tf_op jit(solution)/shard_map/run_experts/pallas_call | solution.py:371
  61.0 1.5 collective-permute-done.1.refs_2_.refs_4_
  62.5 2.2 %collective-permute-start.14 = (bf16[48,1536]{1,0:T(8,128)(2,1)S(1)}, bf16[48,1536]{1,0:T(8,128)(2,1)S(1)}, u32[]{:S(2)}, u32[]{:S(2)}) collective-permute-start(bf16[48,1536]{1,0:T(8,128)(2,1)S(1)} %get-tuple-element.66), channel_id=1, source_target_pairs={{0,5},{1,4},{2,7},{3,6},{4,1},{5,0},{6,3},{7,2},{8,13},{9,12},{10,... | collective-permute-start | bytes 442376 | tf_op jit(solution)/shard_map/ppermute | solution.py:584
  64.7 2.5 %collective-permute-done.2.refs_3_.refs_5_ = bf16[96,1536]{1,0:T(8,128)(2,1)S(1)} collective-permute-done((bf16[96,1536]{1,0:T(8,128)(2,1)S(1)}, bf16[96,1536]{1,0:T(8,128)(2,1)S(1)}, u32[]{:S(2)}, u32[]{:S(2)}) %collective-permute-start.2) | collective-permute-done | bytes 294944 | tf_op jit(solution)/shard_map/ppermute | solution.py:584
  67.2 4.0 %collective-permute-start.16 = (bf16[48,1536]{1,0:T(8,128)(2,1)S(1)}, bf16[48,1536]{1,0:T(8,128)(2,1)S(1)}, u32[]{:S(2)}, u32[]{:S(2)}) collective-permute-start(bf16[48,1536]{1,0:T(8,128)(2,1)S(1)} %get-tuple-element.68), channel_id=1, source_target_pairs={{0,7},{1,6},{2,5},{3,4},{4,3},{5,2},{6,1},{7,0},{8,15},{9,14},{10,... | collective-permute-start | bytes 442376 | tf_op jit(solution)/shard_map/ppermute | solution.py:584
  71.2 1.5 collective-permute-start.21
  72.7 5.0 %collective-permute-done.13.refs_4_ = bf16[48,1536]{1,0:T(8,128)(2,1)S(1)} collective-permute-done((bf16[48,1536]{1,0:T(8,128)(2,1)S(1)}, bf16[48,1536]{1,0:T(8,128)(2,1)S(1)}, u32[]{:S(2)}, u32[]{:S(2)}) %collective-permute-start.13) | collective-permute-done | bytes 147488 | tf_op jit(solution)/shard_map/ppermute | solution.py:584
  77.7 2.4 %collective-permute-done.14.refs_5_ = bf16[48,1536]{1,0:T(8,128)(2,1)S(1)} collective-permute-done((bf16[48,1536]{1,0:T(8,128)(2,1)S(1)}, bf16[48,1536]{1,0:T(8,128)(2,1)S(1)}, u32[]{:S(2)}, u32[]{:S(2)}) %collective-permute-start.14) | collective-permute-done | bytes 147488 | tf_op jit(solution)/shard_map/ppermute | solution.py:584
  80.0 1.6 collective-permute-start.30
  81.8 3.3 %run_experts.2 = (bf16[240,768]{1,0:T(8,128)(2,1)S(1)}, bf16[240,768]{1,0:T(8,128)(2,1)S(1)}, bf16[48,1536]{1,0:T(8,128)(2,1)S(1)}, bf16[48,1536]{1,0:T(8,128)(2...) custom-call(bf16[96,1536]{1,0:T(8,128)(2,1)S(1)} %get-tuple-element.49.refs_0_.ref, ...), custom_call_target="tpu_custom_call" | custom-call | tf_op jit(solution)/shard_map/run_experts/pallas_call | solution.py:371
  85.1 3.5 %collective-permute-start.15 = (bf16[48,1536]{1,0:T(8,128)(2,1)S(1)}, bf16[48,1536]{1,0:T(8,128)(2,1)S(1)}, u32[]{:S(2)}, u32[]{:S(2)}) collective-permute-start(bf16[48,1536]{1,0:T(8,128)(2,1)S(1)} %get-tuple-element.67), channel_id=1, source_target_pairs={{0,6},{1,7},{2,4},{3,5},{4,2},{5,3},{6,0},{7,1},{8,14},{9,15},{10,... | collective-permute-start | bytes 442376 | tf_op jit(solution)/shard_map/ppermute | solution.py:584
  88.6 1.5 collective-permute-start.4
  91.6 3.4 %collective-permute-start.5 = (bf16[48,1536]{1,0:T(8,128)(2,1)S(1)}, bf16[48,1536]{1,0:T(8,128)(2,1)S(1)}, u32[]{:S(2)}, u32[]{:S(2)}) collective-permute-start(bf16[48,1536]{1,0:T(8,128)(2,1)S(1)} %get-tuple-element.56), channel_id=1, source_target_pairs={{0,2},{1,3},{2,0},{3,1},{4,6},{5,7},{6,4},{7,5},{8,10},{9,11},{10,... | collective-permute-start | bytes 442376 | tf_op jit(solution)/shard_map/ppermute | solution.py:584
  96.3 1.1 weight_terms.5
  97.7 1.8 %collective-permute-done.5.refs_2_ = bf16[48,1536]{1,0:T(8,128)(2,1)S(1)} collective-permute-done((bf16[48,1536]{1,0:T(8,128)(2,1)S(1)}, bf16[48,1536]{1,0:T(8,128)(2,1)S(1)}, u32[]{:S(2)}, u32[]{:S(2)}) %collective-permute-start.5) | collective-permute-done | bytes 147488 | tf_op jit(solution)/shard_map/ppermute | solution.py:584
  99.5 2.3 %collective-permute-start.6 = (bf16[48,1536]{1,0:T(8,128)(2,1)S(1)}, bf16[48,1536]{1,0:T(8,128)(2,1)S(1)}, u32[]{:S(2)}, u32[]{:S(2)}) collective-permute-start(bf16[48,1536]{1,0:T(8,128)(2,1)S(1)} %get-tuple-element.57), channel_id=1, source_target_pairs={{0,3},{1,2},{2,1},{3,0},{4,7},{5,6},{6,5},{7,4},{8,11},{9,10},{10,... | collective-permute-start | bytes 442376 | tf_op jit(solution)/shard_map/ppermute | solution.py:584
  101.8 4.3 %collective-permute-done.6.refs_3_ = bf16[48,1536]{1,0:T(8,128)(2,1)S(1)} collective-permute-done((bf16[48,1536]{1,0:T(8,128)(2,1)S(1)}, bf16[48,1536]{1,0:T(8,128)(2,1)S(1)}, u32[]{:S(2)}, u32[]{:S(2)}) %collective-permute-start.6) | collective-permute-done | bytes 147488 | tf_op jit(solution)/shard_map/ppermute | solution.py:584
  106.4 2.2 %collective-permute-start.33 = (bf16[128,1024]{1,0:T(8,128)(2,1)S(1)}, bf16[128,1024]{1,0:T(8,128)(2,1)S(1)}, u32[]{:S(2)}, u32[]{:S(2)}) collective-permute-start(bf16[128,1024]{1,0:T(8,128)(2,1)S(1)} %add_back.3.refs_0_.refs_2_), channel_id=1, source_target_pairs={{0,16},{8,24},{16,0},{24,8},{1,17},{9,25},{17,1},{25,9},{2,18},{10... | collective-permute-start | bytes 786440 | tf_op jit(solution)/shard_map/ppermute | solution.py:584
  109.8 1.1 weight_terms.4
  111.7 6.7 %collective-permute-done.27.refs_4_ = bf16[128,512]{1,0:T(8,128)(2,1)S(1)} collective-permute-done((bf16[128,512]{1,0:T(8,128)(2,1)S(1)}, bf16[128,512]{1,0:T(8,128)(2,1)S(1)}, u32[]{:S(2)}, u32[]{:S(2)}) %collective-permute-start.27) | collective-permute-done | bytes 131104 | tf_op jit(solution)/shard_map/ppermute | solution.py:584
  119.7 1.3 collective-permute-done.19.refs_3_.refs_13_
  121.5 1.7 %collective-permute-start.42 = (bf16[192,1536]{1,0:T(8,128)(2,1)S(1)}, bf16[192,1536]{1,0:T(8,128)(2,1)S(1)}, u32[]{:S(2)}, u32[]{:S(2)}) collective-permute-start(bf16[192,1536]{1,0:T(8,128)(2,1)S(1)} %add_convert_fusion.1), channel_id=1, source_target_pairs={{0,16},{8,24},{16,0},{24,8},{1,17},{9,25},{17,1},{25,9},{2,18},{10... | collective-permute-start | bytes 1769480 | tf_op jit(solution)/shard_map/ppermute | solution.py:584
  123.8 1.6 %collective-permute-start.39 = (bf16[192,768]{1,0:T(8,128)(2,1)S(1)}, bf16[192,768]{1,0:T(8,128)(2,1)S(1)}, u32[]{:S(2)}, u32[]{:S(2)}) collective-permute-start(bf16[192,768]{1,0:T(8,128)(2,1)S(1)} %add_convert_fusion.3), channel_id=1, source_target_pairs={{0,16},{8,24},{16,0},{24,8},{1,17},{9,25},{17,1},{25,9},{2,18},{10... | collective-permute-start | bytes 884744 | tf_op jit(solution)/shard_map/ppermute | solution.py:584
  125.4 4.3 %probabilities.1 = (bf16[12,128,512]{2,1,0:T(8,128)(2,1)S(1)}, bf16[12,128,512]{2,1,0:T(8,128)(2,1)S(1)}) custom-call(bf16[128,1536]{1,0:T(8,128)(2,1)S(1)} %bitcast.50, bf16[128,1536]{1,0:T(8,128)(2,1)S(1)} %collective-permute-done.17.refs_1_.refs_11_, bf16[128,1536]{1,0:T(8,128)(2,1)S(1)} %collective-permute-done.18.refs_2_.refs_12_, ...), custom_call_target="tpu_custom_call" | custom-call | tf_op jit(solution)/shard_map/probabilities/pallas_call | solution.py:495
  129.8 2.9 %query_side.2.refs_11_ = bf16[128,1536]{1,0:T(8,128)(2,1)} custom-call(bf16[128,1024]{1,0:T(8,128)(2,1)S(1)} %add_back.3.refs_0_.refs_2_, bf16[128,1536]{1,0:T(8,128)(2,1)S(1)} %bitcast.27, bf16[12,128,512]{2,1,0:T(8,128)(2,1)S(1)} %get-tuple-element.69.refs_2_, bf16[128,1536]{1,0:T(8,128)(2,1)S(1)} %bitcast.46, ...), custom_call_target="tpu_custom_call" | custom-call | tf_op jit(solution)/shard_map/query_side/pallas_call | solution.py:526
  132.7 1.7 %query_side.3 = bf16[128,1536]{1,0:T(8,128)(2,1)} custom-call(bf16[128,512]{1,0:T(8,128)(2,1)S(1)} %add_back.2.refs_0_.refs_2_, bf16[128,1536]{1,0:T(8,128)(2,1)S(1)} %bitcast.28, bf16[12,128,512]{2,1,0:T(8,128)(2,1)S(1)} %get-tuple-element.69.refs_2_, bf16[128,1536]{1,0:T(8,128)(2,1)S(1)} %bitcast.47, ...), custom_call_target="tpu_custom_call", output_to_operand_aliasing={{}: (11, {})} | custom-call | tf_op jit(solution)/shard_map/query_side/pallas_call | solution.py:526
  134.4 9.7 %collective-permute-done.37 = bf16[192,768]{1,0:T(8,128)(2,1)S(1)} collective-permute-done((bf16[192,768]{1,0:T(8,128)(2,1)S(1)}, bf16[192,768]{1,0:T(8,128)(2,1)S(1)}, u32[]{:S(2)}, u32[]{:S(2)}) %collective-permute-start.37) | collective-permute-done | bytes 294944 | tf_op jit(solution)/shard_map/ppermute | solution.py:584
  144.0 5.5 %collective-permute-done.39 = bf16[192,768]{1,0:T(8,128)(2,1)S(1)} collective-permute-done((bf16[192,768]{1,0:T(8,128)(2,1)S(1)}, bf16[192,768]{1,0:T(8,128)(2,1)S(1)}, u32[]{:S(2)}, u32[]{:S(2)}) %collective-permute-start.39) | collective-permute-done | bytes 294944 | tf_op jit(solution)/shard_map/ppermute | solution.py:584
  150.0 1.0 fusion
  151.2 3.3 %key_side.2 = (bf16[128,1536]{1,0:T(8,128)(2,1)}, bf16[128,1536]{1,0:T(8,128)(2,1)}) custom-call(bf16[12,128,512]{2,1,0:T(8,128)(2,1)S(1)} %get-tuple-element.70.refs_0_, bf16[128,1536]{1,0:T(8,128)(2,1)S(1)} %bitcast.37, bf16[128,1024]{1,0:T(8,128)(2,1)S(1)} %add_back.3.refs_0_.refs_2_, bf16[128,1024]{1,0:T(8,128)(2,1)S(1)} %collective-permute-done.32.refs_3_, ...), custom_call_target="tpu_custom_call" | custom-call | tf_op jit(solution)/shard_map/key_side/pallas_call | solution.py:567
  154.6 1.8 %key_side.3 = (bf16[128,1536]{1,0:T(8,128)(2,1)}, bf16[128,1536]{1,0:T(8,128)(2,1)}) custom-call(bf16[12,128,512]{2,1,0:T(8,128)(2,1)S(1)} %get-tuple-element.70.refs_0_, bf16[128,1536]{1,0:T(8,128)(2,1)S(1)} %bitcast.38, bf16[128,512]{1,0:T(8,128)(2,1)S(1)} %add_back.2.refs_0_.refs_2_, ...), custom_call_target="tpu_custom_call", output_to_operand_aliasing={{0}: (14, {}), {1}: (15, {})} | custom-call | tf_op jit(solution)/shard_map/key_side/pallas_call | solution.py:567
  156.4 1.0 fusion.1
  (87 shorter events, 14.3 us)
Async XLA Ops:
  4.0 48.5 %copy-start.11 = (bf16[1,128,1536]{2,1,0:T(8,128)(2,1)S(1)}, bf16[1,128,1536]{2,1,0:T(8,128)(2,1)}, u32[]{:S(2)}) copy-start(bf16[1,128,1536]{2,1,0:T(8,128)(2,1)} %param.9) | copy-start | bytes 1179652
  7.6 10.9 %collective-permute-start.10 = (bf16[48,1536]{1,0:T(8,128)(2,1)S(1)}, bf16[48,1536]{1,0:T(8,128)(2,1)S(1)}, u32[]{:S(2)}, u32[]{:S(2)}) collective-permute-start(bf16[48,1536]{1,0:T(8,128)(2,1)S(1)} %get-tuple-element.61), channel_id=1, source_target_pairs={{0,7},{1,6},{2,5},{3,4},{4,3},{5,2},{6,1},{7,0},{8,15},{9,14},{10,... | collective-permute-start | bytes 442376 | tf_op jit(solution)/shard_map/ppermute | solution.py:584
  13.7 22.8 %collective-permute-start.11 = (bf16[48,1536]{1,0:T(8,128)(2,1)S(1)}, bf16[48,1536]{1,0:T(8,128)(2,1)S(1)}, u32[]{:S(2)}, u32[]{:S(2)}) collective-permute-start(bf16[48,1536]{1,0:T(8,128)(2,1)S(1)} %get-tuple-element.62), channel_id=1, source_target_pairs={{0,4},{1,5},{2,6},{3,7},{4,0},{5,1},{6,2},{7,3},{8,12},{9,13},{10,... | collective-permute-start | bytes 442376 | tf_op jit(solution)/shard_map/ppermute | solution.py:584
  13.7 27.7 %collective-permute-start.12 = (bf16[48,1536]{1,0:T(8,128)(2,1)S(1)}, bf16[48,1536]{1,0:T(8,128)(2,1)S(1)}, u32[]{:S(2)}, u32[]{:S(2)}) collective-permute-start(bf16[48,1536]{1,0:T(8,128)(2,1)S(1)} %get-tuple-element.63), channel_id=1, source_target_pairs={{0,5},{1,4},{2,7},{3,6},{4,1},{5,0},{6,3},{7,2},{8,13},{9,12},{10,... | collective-permute-start | bytes 442376 | tf_op jit(solution)/shard_map/ppermute | solution.py:584
  16.6 26.2 %collective-permute-start.7 = (bf16[48,1536]{1,0:T(8,128)(2,1)S(1)}, bf16[48,1536]{1,0:T(8,128)(2,1)S(1)}, u32[]{:S(2)}, u32[]{:S(2)}) collective-permute-start(bf16[48,1536]{1,0:T(8,128)(2,1)S(1)} %get-tuple-element.58), channel_id=1, source_target_pairs={{0,7},{1,6},{2,5},{3,4},{4,3},{5,2},{6,1},{7,0},{8,15},{9,14},{10,... | collective-permute-start | bytes 442376 | tf_op jit(solution)/shard_map/ppermute | solution.py:584
  17.7 31.5 %collective-permute-start.8 = (bf16[48,1536]{1,0:T(8,128)(2,1)S(1)}, bf16[48,1536]{1,0:T(8,128)(2,1)S(1)}, u32[]{:S(2)}, u32[]{:S(2)}) collective-permute-start(bf16[48,1536]{1,0:T(8,128)(2,1)S(1)} %get-tuple-element.59), channel_id=1, source_target_pairs={{0,4},{1,5},{2,6},{3,7},{4,0},{5,1},{6,2},{7,3},{8,12},{9,13},{10,... | collective-permute-start | bytes 442376 | tf_op jit(solution)/shard_map/ppermute | solution.py:584
  18.5 42.3 %collective-permute-start = (bf16[96,1536]{1,0:T(8,128)(2,1)S(1)}, bf16[96,1536]{1,0:T(8,128)(2,1)S(1)}, u32[]{:S(2)}, u32[]{:S(2)}) collective-permute-start(bf16[96,1536]{1,0:T(8,128)(2,1)S(1)} %get-tuple-element.50), channel_id=1, source_target_pairs={{0,1},{1,0},{2,3},{3,2},{4,5},{5,4},{6,7},{7,6},{8,9},{9,8},{10,11... | collective-permute-start | bytes 884744 | tf_op jit(solution)/shard_map/ppermute | solution.py:584
  36.5 15.9 %collective-permute-start.9 = (bf16[48,1536]{1,0:T(8,128)(2,1)S(1)}, bf16[48,1536]{1,0:T(8,128)(2,1)S(1)}, u32[]{:S(2)}, u32[]{:S(2)}) collective-permute-start(bf16[48,1536]{1,0:T(8,128)(2,1)S(1)} %get-tuple-element.60), channel_id=1, source_target_pairs={{0,5},{1,4},{2,7},{3,6},{4,1},{5,0},{6,3},{7,2},{8,13},{9,12},{10,... | collective-permute-start | bytes 442376 | tf_op jit(solution)/shard_map/ppermute | solution.py:584
  41.3 21.1 %collective-permute-start.1 = (bf16[96,1536]{1,0:T(8,128)(2,1)S(1)}, bf16[96,1536]{1,0:T(8,128)(2,1)S(1)}, u32[]{:S(2)}, u32[]{:S(2)}) collective-permute-start(bf16[96,1536]{1,0:T(8,128)(2,1)S(1)} %get-tuple-element.51), channel_id=1, source_target_pairs={{0,2},{1,3},{2,0},{3,1},{4,6},{5,7},{6,4},{7,5},{8,10},{9,11},{10,... | collective-permute-start | bytes 884744 | tf_op jit(solution)/shard_map/ppermute | solution.py:584
  42.8 24.4 %collective-permute-start.2 = (bf16[96,1536]{1,0:T(8,128)(2,1)S(1)}, bf16[96,1536]{1,0:T(8,128)(2,1)S(1)}, u32[]{:S(2)}, u32[]{:S(2)}) collective-permute-start(bf16[96,1536]{1,0:T(8,128)(2,1)S(1)} %get-tuple-element.52), channel_id=1, source_target_pairs={{0,3},{1,2},{2,1},{3,0},{4,7},{5,6},{6,5},{7,4},{8,11},{9,10},{10,... | collective-permute-start | bytes 884744 | tf_op jit(solution)/shard_map/ppermute | solution.py:584
  49.3 21.9 %collective-permute-start.3 = (bf16[96,1536]{1,0:T(8,128)(2,1)S(1)}, bf16[96,1536]{1,0:T(8,128)(2,1)S(1)}, u32[]{:S(2)}, u32[]{:S(2)}) collective-permute-start(bf16[96,1536]{1,0:T(8,128)(2,1)S(1)} %get-tuple-element.53), channel_id=1, source_target_pairs={{0,6},{1,7},{2,4},{3,5},{4,2},{5,3},{6,0},{7,1},{8,14},{9,15},{10,... | collective-permute-start | bytes 884744 | tf_op jit(solution)/shard_map/ppermute | solution.py:584
  52.4 29.2 %collective-permute-start.18 = (bf16[128,1536]{1,0:T(8,128)(2,1)S(1)}, bf16[128,1536]{1,0:T(8,128)(2,1)S(1)}, u32[]{:S(2)}, u32[]{:S(2)}) collective-permute-start(bf16[128,1536]{1,0:T(8,128)(2,1)S(1)} %bitcast.48), channel_id=1, source_target_pairs={{0,16},{8,24},{16,0},{24,8},{1,17},{9,25},{17,1},{25,9},{2,18},{10... | collective-permute-start | bytes 1179656 | tf_op jit(solution)/shard_map/ppermute | solution.py:584
  57.3 13.9 %copy-start.10 = (bf16[1,128,1536]{2,1,0:T(8,128)(2,1)S(1)}, bf16[1,128,1536]{2,1,0:T(8,128)(2,1)}, u32[]{:S(2)}) copy-start(bf16[1,128,1536]{2,1,0:T(8,128)(2,1)} %param.10) | copy-start | bytes 1179652
  57.3 22.8 %copy-start.4 = (bf16[1,128,1536]{2,1,0:T(8,128)(2,1)S(1)}, bf16[1,128,1536]{2,1,0:T(8,128)(2,1)}, u32[]{:S(2)}) copy-start(bf16[1,128,1536]{2,1,0:T(8,128)(2,1)} %param.12) | copy-start | bytes 1179652
  57.3 24.5 %copy-start.1 = (bf16[1,1536,768]{2,1,0:T(8,128)(2,1)S(1)}, bf16[1,1536,768]{2,1,0:T(8,128)(2,1)}, u32[]{:S(2)}) copy-start(bf16[1,1536,768]{2,1,0:T(8,128)(2,1)} %param.16) | copy-start | bytes 7077892
  60.9 16.8 %collective-permute-start.13 = (bf16[48,1536]{1,0:T(8,128)(2,1)S(1)}, bf16[48,1536]{1,0:T(8,128)(2,1)S(1)}, u32[]{:S(2)}, u32[]{:S(2)}) collective-permute-start(bf16[48,1536]{1,0:T(8,128)(2,1)S(1)} %get-tuple-element.65), channel_id=1, source_target_pairs={{0,4},{1,5},{2,6},{3,7},{4,0},{5,1},{6,2},{7,3},{8,12},{9,13},{10,... | collective-permute-start | bytes 442376 | tf_op jit(solution)/shard_map/ppermute | solution.py:584
  62.5 17.6 %collective-permute-start.14 = (bf16[48,1536]{1,0:T(8,128)(2,1)S(1)}, bf16[48,1536]{1,0:T(8,128)(2,1)S(1)}, u32[]{:S(2)}, u32[]{:S(2)}) collective-permute-start(bf16[48,1536]{1,0:T(8,128)(2,1)S(1)} %get-tuple-element.66), channel_id=1, source_target_pairs={{0,5},{1,4},{2,7},{3,6},{4,1},{5,0},{6,3},{7,2},{8,13},{9,12},{10,... | collective-permute-start | bytes 442376 | tf_op jit(solution)/shard_map/ppermute | solution.py:584
  67.2 12.8 %collective-permute-start.16 = (bf16[48,1536]{1,0:T(8,128)(2,1)S(1)}, bf16[48,1536]{1,0:T(8,128)(2,1)S(1)}, u32[]{:S(2)}, u32[]{:S(2)}) collective-permute-start(bf16[48,1536]{1,0:T(8,128)(2,1)S(1)} %get-tuple-element.68), channel_id=1, source_target_pairs={{0,7},{1,6},{2,5},{3,4},{4,3},{5,2},{6,1},{7,0},{8,15},{9,14},{10,... | collective-permute-start | bytes 442376 | tf_op jit(solution)/shard_map/ppermute | solution.py:584
  71.2 13.9 %collective-permute-start.21 = (bf16[128,1536]{1,0:T(8,128)(2,1)S(1)}, bf16[128,1536]{1,0:T(8,128)(2,1)S(1)}, u32[]{:S(2)}, u32[]{:S(2)}) collective-permute-start(bf16[128,1536]{1,0:T(8,128)(2,1)S(1)} %bitcast.43), channel_id=1, source_target_pairs={{0,16},{8,24},{16,0},{24,8},{1,17},{9,25},{17,1},{25,9},{2,18},{10... | collective-permute-start | bytes 1179656 | tf_op jit(solution)/shard_map/ppermute | solution.py:584
  77.7 11.0 %collective-permute-start.17 = (bf16[128,1536]{1,0:T(8,128)(2,1)S(1)}, bf16[128,1536]{1,0:T(8,128)(2,1)S(1)}, u32[]{:S(2)}, u32[]{:S(2)}) collective-permute-start(bf16[128,1536]{1,0:T(8,128)(2,1)S(1)} %bitcast.49), channel_id=1, source_target_pairs={{0,8},{8,0},{16,24},{24,16},{1,9},{9,1},{17,25},{25,17},{2,10},{10... | collective-permute-start | bytes 1179656 | tf_op jit(solution)/shard_map/ppermute | solution.py:584
  80.0 10.1 %collective-permute-start.20 = (bf16[128,1536]{1,0:T(8,128)(2,1)S(1)}, bf16[128,1536]{1,0:T(8,128)(2,1)S(1)}, u32[]{:S(2)}, u32[]{:S(2)}) collective-permute-start(bf16[128,1536]{1,0:T(8,128)(2,1)S(1)} %bitcast.44), channel_id=1, source_target_pairs={{0,8},{8,0},{16,24},{24,16},{1,9},{9,1},{17,25},{25,17},{2,10},{10... | collective-permute-start | bytes 1179656 | tf_op jit(solution)/shard_map/ppermute | solution.py:584
  80.0 11.5 %collective-permute-start.30 = (bf16[128,1536]{1,0:T(8,128)(2,1)S(1)}, bf16[128,1536]{1,0:T(8,128)(2,1)S(1)}, u32[]{:S(2)}, u32[]{:S(2)}) collective-permute-start(bf16[128,1536]{1,0:T(8,128)(2,1)S(1)} %bitcast.25), channel_id=1, source_target_pairs={{0,16},{8,24},{16,0},{24,8},{1,17},{9,25},{17,1},{25,9},{2,18},{10... | collective-permute-start | bytes 1179656 | tf_op jit(solution)/shard_map/ppermute | solution.py:584
  81.6 10.0 %collective-permute-start.29 = (bf16[128,1536]{1,0:T(8,128)(2,1)S(1)}, bf16[128,1536]{1,0:T(8,128)(2,1)S(1)}, u32[]{:S(2)}, u32[]{:S(2)}) collective-permute-start(bf16[128,1536]{1,0:T(8,128)(2,1)S(1)} %bitcast.26), channel_id=1, source_target_pairs={{0,8},{8,0},{16,24},{24,16},{1,9},{9,1},{17,25},{25,17},{2,10},{10... | collective-permute-start | bytes 1179656 | tf_op jit(solution)/shard_map/ppermute | solution.py:584
  85.1 10.8 %collective-permute-start.15 = (bf16[48,1536]{1,0:T(8,128)(2,1)S(1)}, bf16[48,1536]{1,0:T(8,128)(2,1)S(1)}, u32[]{:S(2)}, u32[]{:S(2)}) collective-permute-start(bf16[48,1536]{1,0:T(8,128)(2,1)S(1)} %get-tuple-element.67), channel_id=1, source_target_pairs={{0,6},{1,7},{2,4},{3,5},{4,2},{5,3},{6,0},{7,1},{8,14},{9,15},{10,... | collective-permute-start | bytes 442376 | tf_op jit(solution)/shard_map/ppermute | solution.py:584
  88.6 8.7 %collective-permute-start.4 = (bf16[48,1536]{1,0:T(8,128)(2,1)S(1)}, bf16[48,1536]{1,0:T(8,128)(2,1)S(1)}, u32[]{:S(2)}, u32[]{:S(2)}) collective-permute-start(bf16[48,1536]{1,0:T(8,128)(2,1)S(1)} %get-tuple-element.55), channel_id=1, source_target_pairs={{0,1},{1,0},{2,3},{3,2},{4,5},{5,4},{6,7},{7,6},{8,9},{9,8},{10,11... | collective-permute-start | bytes 442376 | tf_op jit(solution)/shard_map/ppermute | solution.py:584
  90.1 16.3 %collective-permute-start.24 = (bf16[128,1536]{1,0:T(8,128)(2,1)S(1)}, bf16[128,1536]{1,0:T(8,128)(2,1)S(1)}, u32[]{:S(2)}, u32[]{:S(2)}) collective-permute-start(bf16[128,1536]{1,0:T(8,128)(2,1)S(1)} %bitcast.33), channel_id=1, source_target_pairs={{0,16},{8,24},{16,0},{24,8},{1,17},{9,25},{17,1},{25,9},{2,18},{10... | collective-permute-start | bytes 1179656 | tf_op jit(solution)/shard_map/ppermute | solution.py:584
  91.6 17.0 %collective-permute-start.23 = (bf16[128,1536]{1,0:T(8,128)(2,1)S(1)}, bf16[128,1536]{1,0:T(8,128)(2,1)S(1)}, u32[]{:S(2)}, u32[]{:S(2)}) collective-permute-start(bf16[128,1536]{1,0:T(8,128)(2,1)S(1)} %bitcast.34), channel_id=1, source_target_pairs={{0,8},{8,0},{16,24},{24,16},{1,9},{9,1},{17,25},{25,17},{2,10},{10... | collective-permute-start | bytes 1179656 | tf_op jit(solution)/shard_map/ppermute | solution.py:584
  91.6 7.9 %collective-permute-start.5 = (bf16[48,1536]{1,0:T(8,128)(2,1)S(1)}, bf16[48,1536]{1,0:T(8,128)(2,1)S(1)}, u32[]{:S(2)}, u32[]{:S(2)}) collective-permute-start(bf16[48,1536]{1,0:T(8,128)(2,1)S(1)} %get-tuple-element.56), channel_id=1, source_target_pairs={{0,2},{1,3},{2,0},{3,1},{4,6},{5,7},{6,4},{7,5},{8,10},{9,11},{10,... | collective-permute-start | bytes 442376 | tf_op jit(solution)/shard_map/ppermute | solution.py:584
  96.0 23.5 %collective-permute-start.41 = (bf16[192,1536]{1,0:T(8,128)(2,1)S(1)}, bf16[192,1536]{1,0:T(8,128)(2,1)S(1)}, u32[]{:S(2)}, u32[]{:S(2)}) collective-permute-start(bf16[192,1536]{1,0:T(8,128)(2,1)S(1)} %get-tuple-element.88), channel_id=1, source_target_pairs={{0,8},{8,0},{16,24},{24,16},{1,9},{9,1},{17,25},{25,17},{2,10},{10... | collective-permute-start | bytes 1769480 | tf_op jit(solution)/shard_map/ppermute | solution.py:584
  96.3 9.8 %copy-start.9 = (bf16[1,128,1536]{2,1,0:T(8,128)(2,1)S(1)}, bf16[1,128,1536]{2,1,0:T(8,128)(2,1)}, u32[]{:S(2)}) copy-start(bf16[1,128,1536]{2,1,0:T(8,128)(2,1)} %param.13) | copy-start | bytes 1179652
  97.4 13.8 %collective-permute-start.36 = (bf16[192,768]{1,0:T(8,128)(2,1)S(1)}, bf16[192,768]{1,0:T(8,128)(2,1)S(1)}, u32[]{:S(2)}, u32[]{:S(2)}) collective-permute-start(bf16[192,768]{1,0:T(8,128)(2,1)S(1)} %get-tuple-element.80), channel_id=1, source_target_pairs={{0,8},{8,0},{16,24},{24,16},{1,9},{9,1},{17,25},{25,17},{2,10},{10... | collective-permute-start | bytes 884744 | tf_op jit(solution)/shard_map/ppermute | solution.py:584
  99.5 6.6 %collective-permute-start.6 = (bf16[48,1536]{1,0:T(8,128)(2,1)S(1)}, bf16[48,1536]{1,0:T(8,128)(2,1)S(1)}, u32[]{:S(2)}, u32[]{:S(2)}) collective-permute-start(bf16[48,1536]{1,0:T(8,128)(2,1)S(1)} %get-tuple-element.57), channel_id=1, source_target_pairs={{0,3},{1,2},{2,1},{3,0},{4,7},{5,6},{6,5},{7,4},{8,11},{9,10},{10,... | collective-permute-start | bytes 442376 | tf_op jit(solution)/shard_map/ppermute | solution.py:584
  106.1 12.3 %collective-permute-start.38 = (bf16[192,768]{1,0:T(8,128)(2,1)S(1)}, bf16[192,768]{1,0:T(8,128)(2,1)S(1)}, u32[]{:S(2)}, u32[]{:S(2)}) collective-permute-start(bf16[192,768]{1,0:T(8,128)(2,1)S(1)} %get-tuple-element.82), channel_id=1, source_target_pairs={{0,8},{8,0},{16,24},{24,16},{1,9},{9,1},{17,25},{25,17},{2,10},{10... | collective-permute-start | bytes 884744 | tf_op jit(solution)/shard_map/ppermute | solution.py:584
  106.4 12.5 %collective-permute-start.33 = (bf16[128,1024]{1,0:T(8,128)(2,1)S(1)}, bf16[128,1024]{1,0:T(8,128)(2,1)S(1)}, u32[]{:S(2)}, u32[]{:S(2)}) collective-permute-start(bf16[128,1024]{1,0:T(8,128)(2,1)S(1)} %add_back.3.refs_0_.refs_2_), channel_id=1, source_target_pairs={{0,16},{8,24},{16,0},{24,8},{1,17},{9,25},{17,1},{25,9},{2,18},{10... | collective-permute-start | bytes 786440 | tf_op jit(solution)/shard_map/ppermute | solution.py:584
  108.6 10.4 %collective-permute-start.32 = (bf16[128,1024]{1,0:T(8,128)(2,1)S(1)}, bf16[128,1024]{1,0:T(8,128)(2,1)S(1)}, u32[]{:S(2)}, u32[]{:S(2)}) collective-permute-start(bf16[128,1024]{1,0:T(8,128)(2,1)S(1)} %add_back.3.refs_0_.refs_2_), channel_id=1, source_target_pairs={{0,8},{8,0},{16,24},{24,16},{1,9},{9,1},{17,25},{25,17},{2,10},{10... | collective-permute-start | bytes 786440 | tf_op jit(solution)/shard_map/ppermute | solution.py:584
  111.1 7.2 %collective-permute-start.27 = (bf16[128,512]{1,0:T(8,128)(2,1)S(1)}, bf16[128,512]{1,0:T(8,128)(2,1)S(1)}, u32[]{:S(2)}, u32[]{:S(2)}) collective-permute-start(bf16[128,512]{1,0:T(8,128)(2,1)S(1)} %add_back.2.refs_0_.refs_2_), channel_id=1, source_target_pairs={{0,16},{8,24},{16,0},{24,8},{1,17},{9,25},{17,1},{25,9},{2,18},{10... | collective-permute-start | bytes 393224 | tf_op jit(solution)/shard_map/ppermute | solution.py:584
  118.4 31.1 %collective-permute-start.35 = (bf16[384,768]{1,0:T(8,128)(2,1)S(1)}, bf16[384,768]{1,0:T(8,128)(2,1)S(1)}, u32[]{:S(2)}, u32[]{:S(2)}) collective-permute-start(bf16[384,768]{1,0:T(8,128)(2,1)S(1)} %get-tuple-element.78), channel_id=1, source_target_pairs={{0,8},{8,0},{16,24},{24,16},{1,9},{9,1},{17,25},{25,17},{2,10},{10... | collective-permute-start | bytes 1769480 | tf_op jit(solution)/shard_map/ppermute | solution.py:584
  118.4 2.6 %collective-permute-start.19 = (bf16[128,1536]{1,0:T(8,128)(2,1)S(1)}, bf16[128,1536]{1,0:T(8,128)(2,1)S(1)}, u32[]{:S(2)}, u32[]{:S(2)}) collective-permute-start(bf16[128,1536]{1,0:T(8,128)(2,1)S(1)} %collective-permute-done.18.refs_2_.refs_12_), channel_id=1, source_target_pairs={{0,8},{8,0},{16,24},{24,16},{1,9},{9,1},{17,25},{25,17},{2,10},{10... | collective-permute-start | bytes 1179656 | tf_op jit(solution)/shard_map/ppermute | solution.py:584
  118.9 2.6 %collective-permute-start.22 = (bf16[128,1536]{1,0:T(8,128)(2,1)S(1)}, bf16[128,1536]{1,0:T(8,128)(2,1)S(1)}, u32[]{:S(2)}, u32[]{:S(2)}) collective-permute-start(bf16[128,1536]{1,0:T(8,128)(2,1)S(1)} %collective-permute-done.21.refs_6_.refs_5_), channel_id=1, source_target_pairs={{0,8},{8,0},{16,24},{24,16},{1,9},{9,1},{17,25},{25,17},{2,10},{10... | collective-permute-start | bytes 1179656 | tf_op jit(solution)/shard_map/ppermute | solution.py:584
  119.0 4.4 %collective-permute-start.31 = (bf16[128,1536]{1,0:T(8,128)(2,1)S(1)}, bf16[128,1536]{1,0:T(8,128)(2,1)S(1)}, u32[]{:S(2)}, u32[]{:S(2)}) collective-permute-start(bf16[128,1536]{1,0:T(8,128)(2,1)S(1)} %collective-permute-done.30.refs_8_), channel_id=1, source_target_pairs={{0,8},{8,0},{16,24},{24,16},{1,9},{9,1},{17,25},{25,17},{2,10},{10... | collective-permute-start | bytes 1179656 | tf_op jit(solution)/shard_map/ppermute | solution.py:584
  119.4 4.4 %collective-permute-start.25 = (bf16[128,1536]{1,0:T(8,128)(2,1)S(1)}, bf16[128,1536]{1,0:T(8,128)(2,1)S(1)}, u32[]{:S(2)}, u32[]{:S(2)}) collective-permute-start(bf16[128,1536]{1,0:T(8,128)(2,1)S(1)} %collective-permute-done.24.refs_9_), channel_id=1, source_target_pairs={{0,8},{8,0},{16,24},{24,16},{1,9},{9,1},{17,25},{25,17},{2,10},{10... | collective-permute-start | bytes 1179656 | tf_op jit(solution)/shard_map/ppermute | solution.py:584
  120.9 35.5 %collective-permute-start.40 = (bf16[192,1536]{1,0:T(8,128)(2,1)S(1)}, bf16[192,1536]{1,0:T(8,128)(2,1)S(1)}, u32[]{:S(2)}, u32[]{:S(2)}) collective-permute-start(bf16[192,1536]{1,0:T(8,128)(2,1)S(1)} %get-tuple-element.86), channel_id=1, source_target_pairs={{0,8},{8,0},{16,24},{24,16},{1,9},{9,1},{17,25},{25,17},{2,10},{10... | collective-permute-start | bytes 1769480 | tf_op jit(solution)/shard_map/ppermute | solution.py:584
  121.5 34.9 %collective-permute-start.42 = (bf16[192,1536]{1,0:T(8,128)(2,1)S(1)}, bf16[192,1536]{1,0:T(8,128)(2,1)S(1)}, u32[]{:S(2)}, u32[]{:S(2)}) collective-permute-start(bf16[192,1536]{1,0:T(8,128)(2,1)S(1)} %add_convert_fusion.1), channel_id=1, source_target_pairs={{0,16},{8,24},{16,0},{24,8},{1,17},{9,25},{17,1},{25,9},{2,18},{10... | collective-permute-start | bytes 1769480 | tf_op jit(solution)/shard_map/ppermute | solution.py:584
  123.3 20.7 %collective-permute-start.37 = (bf16[192,768]{1,0:T(8,128)(2,1)S(1)}, bf16[192,768]{1,0:T(8,128)(2,1)S(1)}, u32[]{:S(2)}, u32[]{:S(2)}) collective-permute-start(bf16[192,768]{1,0:T(8,128)(2,1)S(1)} %add_convert_fusion.4), channel_id=1, source_target_pairs={{0,16},{8,24},{16,0},{24,8},{1,17},{9,25},{17,1},{25,9},{2,18},{10... | collective-permute-start | bytes 884744 | tf_op jit(solution)/shard_map/ppermute | solution.py:584
  123.8 25.7 %collective-permute-start.39 = (bf16[192,768]{1,0:T(8,128)(2,1)S(1)}, bf16[192,768]{1,0:T(8,128)(2,1)S(1)}, u32[]{:S(2)}, u32[]{:S(2)}) collective-permute-start(bf16[192,768]{1,0:T(8,128)(2,1)S(1)} %add_convert_fusion.3), channel_id=1, source_target_pairs={{0,16},{8,24},{16,0},{24,8},{1,17},{9,25},{17,1},{25,9},{2,18},{10... | collective-permute-start | bytes 884744 | tf_op jit(solution)/shard_map/ppermute | solution.py:584
  144.0 10.5 %collective-permute-start.26 = (bf16[128,512]{1,0:T(8,128)(2,1)S(1)}, bf16[128,512]{1,0:T(8,128)(2,1)S(1)}, u32[]{:S(2)}, u32[]{:S(2)}) collective-permute-start(bf16[128,512]{1,0:T(8,128)(2,1)S(1)} %add_back.2.refs_0_.refs_2_), channel_id=1, source_target_pairs={{0,8},{8,0},{16,24},{24,16},{1,9},{9,1},{17,25},{25,17},{2,10},{10... | collective-permute-start | bytes 393224 | tf_op jit(solution)/shard_map/ppermute | solution.py:584
  149.5 5.1 %collective-permute-start.28 = (bf16[128,512]{1,0:T(8,128)(2,1)S(1)}, bf16[128,512]{1,0:T(8,128)(2,1)S(1)}, u32[]{:S(2)}, u32[]{:S(2)}) collective-permute-start(bf16[128,512]{1,0:T(8,128)(2,1)S(1)} %collective-permute-done.27.refs_4_), channel_id=1, source_target_pairs={{0,8},{8,0},{16,24},{24,16},{1,9},{9,1},{17,25},{25,17},{2,10},{10... | collective-permute-start | bytes 393224 | tf_op jit(solution)/shard_map/ppermute | solution.py:584
  149.5 1.7 %collective-permute-start.34 = (bf16[128,1024]{1,0:T(8,128)(2,1)S(1)}, bf16[128,1024]{1,0:T(8,128)(2,1)S(1)}, u32[]{:S(2)}, u32[]{:S(2)}) collective-permute-start(bf16[128,1024]{1,0:T(8,128)(2,1)S(1)} %collective-permute-done.33.refs_4_), channel_id=1, source_target_pairs={{0,8},{8,0},{16,24},{24,16},{1,9},{9,1},{17,25},{25,17},{2,10},{10... | collective-permute-start | bytes 786440 | tf_op jit(solution)/shard_map/ppermute | solution.py:584
  (9 other events, 17.1 us)
